TPU v7x, 32 devices: a whole 2x2x4 slice. The times are simulated.
32 devices in a mesh: section: 16 (over z, y, x), dp: 2 (over core).
Axes of the slice: x: 2, y: 2, z: 4, core: 2. Of those that a mesh axis runs over, the one named last changes fastest.
Arguments:
- pipe_maps: bfloat16 [16, 2, 8, 32, 384], P('section', 'dp'), may hold values from -6 to 6
- fresh_maps: bfloat16 [3, 2, 8, 32, 384], P(None, 'dp'), may hold values from -6 to 6
- teacher_weight: bfloat16 [32, 3, 3, 384, 384], P('section'), may hold values from -0.109375 to 0.109375
- student_depth: float32 [32, 49, 384], P('section'), may hold values from -0.875 to 0.875
- student_point: bfloat16 [32, 384, 384], P('section'), may hold values from -0.3125 to 0.3125
Outputs:
- final_maps: bfloat16 [16, 2, 8, 32, 384], P('section', 'dp')
- point_grad: float32 [32, 384, 384], P('section', None, 'dp')
- depth_grad: float32 [32, 49, 384], P('section', None, 'dp')
All inputs are finite; a program needn't handle non-finite values.
Results may differ from a plain program's by a relative error of at most 0.012.
Values may be sent and summed in bfloat16 or wider, within the bound.
A program may use at most 128 MiB of HBM per device.

v0:
```python
import functools

import jax
import jax.numpy as jnp
from jax import lax
from jax.experimental import pallas as pl
from jax.experimental.pallas import tpu as pltpu
from jax.sharding import PartitionSpec as P

LANES = 128
F32 = jnp.float32
BF16 = jnp.bfloat16
MESH = pl.DeviceIdType.MESH
NT = (((1,), (1,)), ((), ()))


def gather_windows(vals, win_ref, height):
    rows, chans = vals.shape
    pair = 2 * height
    h_of = lax.rem(lax.broadcasted_iota(jnp.int32, (rows, chans), 0), height)
    zero = jnp.zeros((height, chans), F32)
    cube = vals.reshape(rows // height, height, chans)
    for row in range(3):
        dy = row - 1
        moved = vals
        if dy:
            moved = pltpu.roll(cube, (-dy) % height, 1).reshape(rows, chans)
            moved = jnp.where((h_of + dy >= 0) & (h_of + dy < height), moved, 0.0)
        for col in range(3):
            if col == 0:
                part = jnp.concatenate([zero, moved[rows - pair : rows - height], moved[: rows - pair]], axis=0)
            elif col == 2:
                part = jnp.concatenate([moved[pair:], moved[height:pair], zero], axis=0)
            else:
                part = moved
            tap = row * 3 + col
            win_ref[:, tap * chans : (tap + 1) * chans] = part.astype(BF16)


def teacher_kernel(height, lead_ref, fresh_ref, relay_ref, weight_ref, teach_ref, cur_ref, win_ref):
    lead = lead_ref[0] == 1
    current = jnp.where(lead, fresh_ref[...].astype(F32), relay_ref[...].astype(F32))
    cur_ref[...] = current.astype(BF16)
    gather_windows(current, win_ref, height)
    hidden = jnp.dot(win_ref[...], weight_ref[0], preferred_element_type=F32)
    gather_windows(jnp.maximum(hidden, 0.0), win_ref, height)
    second = jnp.dot(win_ref[...], weight_ref[1], preferred_element_type=F32)
    teach_ref[...] = (0.8 * (current + second)).astype(BF16)


def teacher(lead, fresh, relay, weight, height):
    rows, chans = fresh.shape
    vmem = pl.BlockSpec(memory_space=pltpu.VMEM)
    return pl.pallas_call(
        functools.partial(teacher_kernel, height),
        out_shape=(jax.ShapeDtypeStruct((rows, chans), BF16),) * 2,
        in_specs=[pl.BlockSpec(memory_space=pltpu.SMEM), vmem, vmem, vmem],
        out_specs=(vmem, vmem),
        scratch_shapes=[pltpu.VMEM((rows, 9 * chans), BF16)],
        compiler_params=pltpu.CompilerParams(vmem_limit_bytes=12 << 20),
        cost_estimate=pl.CostEstimate(
            flops=2 * 2 * 9 * rows * chans * chans, bytes_accessed=weight.size * 2, transcendentals=0
        ),
        name="teacher",
    )(lead, fresh, relay, weight)


def spread(vals, out_ref, block, height):
    pair = vals.reshape(-1, 2 * height, LANES)
    low, high = pair[:, :height], pair[:, height:]
    h_of = lax.broadcasted_iota(jnp.int32, low.shape, 1)
    zero = jnp.zeros((3, height, LANES), F32)
    for row in range(7):
        dy = row - 3
        one, two = low, high
        if dy:
            keep = (h_of + dy >= 0) & (h_of + dy < height)
            one = jnp.where(keep, pltpu.roll(low, (-dy) % height, 1), 0.0)
            two = jnp.where(keep, pltpu.roll(high, (-dy) % height, 1), 0.0)
        left = jnp.concatenate([zero, one, two[:3]], axis=0)
        right = jnp.concatenate([one[-3:], two, zero], axis=0)
        out_ref[block, row] = jnp.concatenate([left, right], axis=1)


def columns(block):
    return pl.ds(pl.multiple_of(block * LANES, LANES), LANES)


def tap_sum(src_ref, block, taps_ref, which, start, count, flip):
    total, held = None, None
    for row in range(7):
        strip = src_ref[block, row, pl.ds(start, count + 6)].astype(BF16)
        terms = []
        for col in range(7):
            tap = row * 7 + col
            tap = 48 - tap if flip else tap
            coef = jnp.broadcast_to(taps_ref[which, tap : tap + 1, columns(block)], strip.shape[1:])
            terms.append(strip[col : col + count] * coef.astype(BF16)[None])
        while len(terms) > 1:
            terms = [sum(terms[i + 1 : i + 2], terms[i]) for i in range(0, len(terms), 2)]
        if held is None and row < 6:
            held = terms[0]
            continue
        part = terms[0] if held is None else held + terms[0]
        held = None
        total = part.astype(F32) if total is None else total + part.astype(F32)
    return total


def gelu_pair(act):
    root = 0.7978845608028654
    square = act * act
    tanh = jnp.tanh(root * (act + 0.044715 * square * act))
    half = 0.5 * (1.0 + tanh)
    slope = half + 0.5 * act * (1.0 - tanh * tanh) * (root * (1.0 + 3.0 * 0.044715 * square))
    return act * half, slope


def student_kernel(
    height, step, sections, cur_ref, teach_ref, taps_ref, point_ref,
    gel0, gel1, grad0, grad1, dk_ref, *rest,
):
    if sections:
        relay_ref, *rest = rest
        *rest, land, send_sem, recv_sem = rest
        spot = lax.axis_index("section")
        later, earlier = lax.rem(spot + 1, sections), lax.rem(spot + sections - 1, sections)
        barrier = pltpu.get_barrier_semaphore()

        @pl.when(spot > 0)
        def _():
            pl.semaphore_signal(barrier, inc=1, device_id={"section": earlier}, device_id_type=MESH)

        copy = pltpu.make_async_remote_copy(
            src_ref=teach_ref,
            dst_ref=land,
            send_sem=send_sem,
            recv_sem=recv_sem,
            device_id={"section": later},
            device_id_type=MESH,
        )
    src0, src1, src2, slope0, slope1, dact, u_one_ref, resid_ref, sums_ref = rest
    gels, grads = (gel0, gel1), (grad0, grad1)
    rows, chans = cur_ref.shape
    blocks = chans // LANES
    pair = 2 * height
    chunks = rows // (pair * step)
    srcs, slopes = (src0, src1), (slope0, slope1)

    def lanes(block):
        return slice(block * LANES, (block + 1) * LANES)

    def span(index):
        return pl.ds(pl.multiple_of(index * step * pair, step * pair), step * pair)

    for block in range(blocks):
        spread(cur_ref[:, lanes(block)].astype(F32), src0, block, height)

    def forward(which):
        def chunk(at, carry):
            block, index = at // chunks, lax.rem(at, chunks)
            act = tap_sum(srcs[which], block, taps_ref, which, index * step, step, False)
            gel, slope = gelu_pair(act.reshape(step * pair, LANES))
            slopes[which][span(index), columns(block)] = slope
            gels[which][span(index), columns(block)] = gel.astype(BF16)
            return carry

        lax.fori_loop(0, blocks * chunks, chunk, 0)
        return jnp.dot(gels[which][...], point_ref[which], preferred_element_type=F32)

    u_one_ref[...] = forward(0) + cur_ref[...].astype(F32)
    for block in range(blocks):
        spread(u_one_ref[:, lanes(block)], src1, block, height)
    if sections:

        @pl.when(spot < sections - 1)
        def _():
            pl.semaphore_wait(barrier, 1)
            copy.start()

    diff = forward(1) + u_one_ref[...] - teach_ref[...].astype(F32)
    resid = diff * (4.0 / rows)
    resid_ref[...] = resid
    grad1[...] = resid.astype(BF16)

    def taps_grad(which):
        def over_rows(at, carry):
            block, row = at // 7, lax.rem(at, 7)
            strip = srcs[which][block, row].astype(BF16)
            part = dact[:, columns(block)].reshape(-1, pair, LANES).astype(BF16)
            count = part.shape[0]
            for col in range(7):
                prod = strip[col : col + count] * part
                size = count
                while size > 1:
                    size //= 2
                    prod = prod[:size] + prod[size:]
                wide = prod[0].astype(F32)
                sums_ref[block, row, col] = wide[:height] + wide[height:]
            return carry

        lax.fori_loop(0, 7 * blocks, over_rows, 0)
        for block in range(blocks):
            for row in range(7):
                dk_ref[which, block, row] = jnp.sum(sums_ref[block, row], axis=1)

    def back_point(which):
        dgel = lax.dot_general(grads[which][...], point_ref[which], NT, preferred_element_type=F32)
        return dgel * slopes[which][...]

    dact_one = back_point(1)
    dact[...] = dact_one
    for block in range(blocks):
        spread(dact_one[:, lanes(block)], src2, block, height)

    def chunk_back(at, carry):
        block, index = at // chunks, lax.rem(at, chunks)
        back = tap_sum(src2, block, taps_ref, 1, index * step, step, True)
        back = back.reshape(step * pair, LANES) + resid_ref[span(index), columns(block)]
        grad0[span(index), columns(block)] = back.astype(BF16)
        return carry

    lax.fori_loop(0, blocks * chunks, chunk_back, 0)
    taps_grad(1)
    dact[...] = back_point(0)
    taps_grad(0)
    if sections:

        @pl.when(spot > 0)
        def _():
            copy.wait_recv()
            relay_ref[...] = land[...]

        @pl.when(spot == 0)
        def _():
            relay_ref[...] = jnp.zeros_like(relay_ref)

        @pl.when(spot < sections - 1)
        def _():
            copy.wait_send()


def student(current, teach, taps, point, height, sections):
    rows, chans = current.shape
    blocks = chans // LANES
    half = rows // (2 * height)
    vmem = pl.BlockSpec(memory_space=pltpu.VMEM)
    spread_shape = pltpu.VMEM((blocks, 7, half + 6, 2 * height, LANES), F32)
    map_shape = pltpu.VMEM((rows, chans), F32)
    flat = jax.ShapeDtypeStruct((rows, chans), BF16)
    outs = [flat] * 4 + [jax.ShapeDtypeStruct((2, blocks, 7, 7, LANES), F32)]
    scratch = [spread_shape] * 3 + [map_shape] * 5 + [pltpu.VMEM((blocks, 7, 7, height, LANES), F32)]
    params = {}
    if sections:
        outs.append(flat)
        scratch += [pltpu.VMEM((rows, chans), BF16), pltpu.SemaphoreType.DMA, pltpu.SemaphoreType.DMA]
        params = {"collective_id": 0, "has_side_effects": True}
    return pl.pallas_call(
        functools.partial(student_kernel, height, half // 2, sections),
        out_shape=tuple(outs),
        in_specs=[vmem] * 4,
        out_specs=(vmem,) * len(outs),
        scratch_shapes=scratch,
        compiler_params=pltpu.CompilerParams(vmem_limit_bytes=22 << 20, **params),
        cost_estimate=pl.CostEstimate(
            flops=10_000_000_000, bytes_accessed=8 * rows * chans, transcendentals=0
        ),
        name="student",
    )(current, teach, taps, point)


def body(pipe_maps, fresh_maps, teacher_weight, student_depth, student_point):
    _, _, height, width, chans = pipe_maps.shape
    rows = height * width
    blocks = chans // LANES
    lead = (lax.axis_index("section") == 0).astype(jnp.int32).reshape(1)
    sections = lax.axis_size("section")

    def to_rows(maps):
        front = maps.shape[:-3]
        split = maps.reshape(front + (height, 2, width // 2, chans))
        return jnp.swapaxes(split, -4, -2).reshape(front + (rows, chans))

    relay = to_rows(pipe_maps[0, 0])
    fresh = to_rows(fresh_maps[:, 0])
    weight = teacher_weight.reshape(2, 9 * chans, chans)
    ticks = fresh_maps.shape[0] + 1
    gels, grads, depth_total = [], [], None
    teach = relay
    for tick in range(ticks):
        mine = relay if tick == 0 else fresh[tick - 1]
        teach, current = teacher(lead, mine, relay, weight, height)
        linked = sections if tick + 1 < ticks else 0
        gel0, gel1, grad0, grad1, part, *sent = student(
            current, teach, student_depth, student_point, height, linked
        )
        if sent:
            relay = sent[0]
        gels.append((gel0, gel1))
        grads.append((grad0, grad1))
        depth_total = part if depth_total is None else depth_total + part
    gel_all = [jnp.concatenate([pair[b] for pair in gels]) for b in range(2)]
    grad_all = [jnp.concatenate([pair[b] for pair in grads]) for b in range(2)]
    point_total = [
        lax.dot_general(grad_all[b], gel_all[b], (((0,), (0,)), ((), ())), preferred_element_type=F32)
        for b in range(2)
    ]
    depth_rows = depth_total.transpose(1, 4, 0, 2, 3).reshape(chans, 98)
    packed = jnp.concatenate(point_total + [depth_rows], axis=1)
    parties = lax.axis_size("dp")
    share = chans // parties
    me = lax.axis_index("dp")
    total = lax.dynamic_slice_in_dim(packed, me * share, share, 0)
    for hop in range(1, parties):
        out = lax.dynamic_slice_in_dim(packed, lax.rem(me + hop, parties) * share, share, 0)
        pairs = [(i, (i + hop) % parties) for i in range(parties)]
        total = total + lax.ppermute(out.astype(BF16), "dp", pairs).astype(F32)
    point_grad = jnp.stack([total[:, b * chans : (b + 1) * chans] for b in range(2)]).swapaxes(1, 2)
    depth_grad = total[:, 2 * chans :].T.reshape(2, 49, share)
    final = jnp.swapaxes(teach.reshape(width // 2, 2, height, chans), 0, 2)
    final = final.reshape(1, 1, height, width, chans)
    return final, point_grad, depth_grad


def solution(mesh):
    placed = (
        P("section", "dp", None, None, None),
        P(None, "dp", None, None, None),
        P("section", None, None, None, None),
        P("section", None, None),
        P("section", None, None),
    )
    return jax.shard_map(
        body,
        mesh=mesh,
        in_specs=placed,
        out_specs=(
            P("section", "dp", None, None, None),
            P("section", None, "dp"),
            P("section", None, "dp"),
        ),
        check_vma=False,
    )
```

profile of v0, /device:TPU:25, one launch (start us, length us, event | category | flops | bytes accessed | tf_op | source)
XLA Modules:
  0.0 53.2 jit_solution(14485634176596887140)
XLA Ops:
  0.6 0.0 copy-start.2
  0.6 0.0 copy-start.3
  0.7 1.3 %copy.29 = bf16[3,8,2,16,384]{4,1,2,3,0:T(8,128)(2,1)S(1)} copy(bf16[3,8,2,16,384]{4,3,2,1,0:T(8,128)(2,1)} %bitcast.49) | data formatting | bytes 1179648 | tf_op jit(solution)/shard_map/reshape;squeeze | solution.py:281
  2.0 0.1 fusion.32
  2.0 0.0 copy-done.2
  2.0 0.1 copy.18
  2.1 0.0 copy-done.3
  2.2 0.0 copy-start
  2.2 2.5 %copy-done = bf16[2,3,3,384,384]{4,3,2,1,0:T(8,128)(2,1)S(1)} copy-done((bf16[2,3,3,384,384]{4,3,2,1,0:T(8,128)(2,1)S(1)}, bf16[2,3,3,384,384]{4,3,2,1,0:T(8,128)(2,1)}, u32[]{:S(2)}) %copy-start) | copy-done | bytes 5308440
  4.7 0.0 copy-start.1
  4.7 0.0 slice-start
  4.7 2.4 %teacher.4 = (bf16[256,384]{1,0:T(8,128)(2,1)S(1)}, bf16[256,384]{1,0:T(8,128)(2,1)S(1)}) custom-call(s32[1]{0:T(128)} %bitcast.lead_ref, bf16[256,384]{1,0:T(8,128)(2,1)S(1)} %bitcast.39, bf16[256,384]{1,0:T(8,128)(2,1)S(1)} %bitcast.40, bf16[2,3456,384]{2,1,0:T(8,128)(2,1)S(1)} %bitcast.33), custom_call_target="tpu_custom_call" | custom-call | flops 1358954496 | bytes 5308416 | tf_op jit(solution)/shard_map/teacher/pallas_call | solution.py:54
  7.0 0.0 copy-done.1
  7.1 0.0 slice-start.1
  7.1 8.7 %student.4 = (bf16[256,384]{1,0:T(8,128)(2,1)S(1)}, bf16[256,384]{1,0:T(8,128)(2,1)S(1)}, bf16[256,384]{1,0:T(8,128)(2,1)S(1)}, bf16[256,384]{1,0:T(8,128)(2,1)S...) custom-call(bf16[256,384]{1,0:T(8,128)(2,1)S(1)} %get-tuple-element.34.cur_ref, ...), custom_call_target="tpu_custom_call" | custom-call | flops 10000000000 | bytes 786432 | tf_op jit(solution)/shard_map/student/pallas_call | solution.py:258
  15.7 0.0 slice-done
  15.8 0.0 slice-done.1
  15.8 2.3 %teacher.5 = (bf16[256,384]{1,0:T(8,128)(2,1)S(1)}, bf16[256,384]{1,0:T(8,128)(2,1)S(1)}) custom-call(s32[1]{0:T(128)} %bitcast.lead_ref, bf16[256,384]{1,0:T(8,128)(2,1)S(1)} %bitcast.43, bf16[256,384]{1,0:T(8,128)(2,1)S(1)} %get-tuple-element.36.relay_ref, bf16[2,3456,384]{2,1,0:T(8,128)(2,1)S(1)} %bitcast.36), custom_call_target="tpu_custom_call" | custom-call | flops 1358954496 | bytes 5308416 | tf_op jit(solution)/shard_map/teacher/pallas_call | solution.py:54
  18.1 7.9 %student.5 = (bf16[256,384]{1,0:T(8,128)(2,1)S(1)}, bf16[256,384]{1,0:T(8,128)(2,1)S(1)}, bf16[256,384]{1,0:T(8,128)(2,1)S(1)}, bf16[256,384]{1,0:T(8,128)(2,1)S...) custom-call(bf16[256,384]{1,0:T(8,128)(2,1)S(1)} %get-tuple-element.37.cur_ref, ...), custom_call_target="tpu_custom_call" | custom-call | flops 10000000000 | bytes 786432 | tf_op jit(solution)/shard_map/student/pallas_call | solution.py:258
  26.0 2.3 %teacher.6 = (bf16[256,384]{1,0:T(8,128)(2,1)S(1)}, bf16[256,384]{1,0:T(8,128)(2,1)S(1)}) custom-call(s32[1]{0:T(128)} %bitcast.lead_ref, bf16[256,384]{1,0:T(8,128)(2,1)S(1)} %bitcast.42, bf16[256,384]{1,0:T(8,128)(2,1)S(1)} %get-tuple-element.39.relay_ref, bf16[2,3456,384]{2,1,0:T(8,128)(2,1)S(1)} %bitcast.37), custom_call_target="tpu_custom_call" | custom-call | flops 1358954496 | bytes 5308416 | tf_op jit(solution)/shard_map/teacher/pallas_call | solution.py:54
  28.3 8.1 %student.6 = (bf16[256,384]{1,0:T(8,128)(2,1)S(1)}, bf16[256,384]{1,0:T(8,128)(2,1)S(1)}, bf16[256,384]{1,0:T(8,128)(2,1)S(1)}, bf16[256,384]{1,0:T(8,128)(2,1)S...) custom-call(bf16[256,384]{1,0:T(8,128)(2,1)S(1)} %get-tuple-element.40.cur_ref, ...), custom_call_target="tpu_custom_call" | custom-call | flops 10000000000 | bytes 786432 | tf_op jit(solution)/shard_map/student/pallas_call | solution.py:258
  36.4 2.3 %teacher.7 = (bf16[256,384]{1,0:T(8,128)(2,1)S(1)}, bf16[256,384]{1,0:T(8,128)(2,1)S(1)}) custom-call(s32[1]{0:T(128)} %bitcast.lead_ref, bf16[256,384]{1,0:T(8,128)(2,1)S(1)} %bitcast.41, bf16[256,384]{1,0:T(8,128)(2,1)S(1)} %get-tuple-element.42.relay_ref, bf16[2,3456,384]{2,1,0:T(8,128)(2,1)S(1)} %bitcast.38), custom_call_target="tpu_custom_call" | custom-call | flops 1358954496 | bytes 5308416 | tf_op jit(solution)/shard_map/teacher/pallas_call | solution.py:54
  38.7 7.8 %student.7 = (bf16[256,384]{1,0:T(8,128)(2,1)S(1)}, bf16[256,384]{1,0:T(8,128)(2,1)S(1)}, bf16[256,384]{1,0:T(8,128)(2,1)S(1)}, bf16[256,384]{1,0:T(8,128)(2,1)S(1)}, f32[2,3,7,7,128]{4,3,2,1,0:T(8,128)S(1)}) custom-call(bf16[256,384]{1,0:T(8,128)(2,1)S(1)} %get-tuple-element.47.cur_ref, bf16[256,384]{1,0:T(8,128)(2,1)S(1)} %get-tuple-element.43.teach_ref, ...), custom_call_target="tpu_custom_call" | custom-call | flops 10000000000 | bytes 786432 | tf_op jit(solution)/shard_map/student/pallas_call | solution.py:258
  46.5 0.1 add_bitcast_fusion
  46.5 0.1 copy.24
  46.7 0.6 %fusion.15 = f32[384,384]{0,1:T(8,128)S(1)} fusion(bf16[256,384]{1,0:T(8,128)(2,1)S(1)} %get-tuple-element.56, bf16[256,384]{1,0:T(8,128)(2,1)S(1)} %get-tuple-element.55, bf16[256,384]{1,0:T(8,128)(2,1)S(1)} %get-tuple-element.54, bf16[256,384]{1,0:T(8,128)(2,1)S(1)} %get-tuple-element.53, bf16[256,384]{1,0:T(8,128)(2,1)S(1)} %get-tuple-element.60, ...), kind=kOutput, calls=%fused_computation.18 | convolution fusion | flops 308281344 | bytes 2162688 | tf_op jit(solution)/shard_map/dot_general | solution.py:305
  47.3 0.6 %fusion = f32[384,384]{0,1:T(8,128)S(1)} fusion(bf16[256,384]{1,0:T(8,128)(2,1)S(1)} %get-tuple-element.48, bf16[256,384]{1,0:T(8,128)(2,1)S(1)} %get-tuple-element.46, bf16[256,384]{1,0:T(8,128)(2,1)S(1)} %get-tuple-element.45, bf16[256,384]{1,0:T(8,128)(2,1)S(1)} %get-tuple-element.44, bf16[256,384]{1,0:T(8,128)(2,1)S(1)} %get-tuple-element.52, ...), kind=kOutput, calls=%fused_computation.3 | convolution fusion | flops 308281344 | bytes 2162688 | tf_op jit(solution)/shard_map/dot_general | solution.py:305
  47.9 0.1 pad_maximum_fusion
  48.0 0.2 dynamic-slice_convert_fusion
  48.2 1.4 %collective-permute-start = (bf16[192,866]{0,1:T(8,128)(2,1)S(1)}, bf16[192,866]{0,1:T(8,128)(2,1)S(1)}, u32[]{:S(2)}, u32[]{:S(2)}) collective-permute-start(bf16[192,866]{0,1:T(8,128)(2,1)S(1)} %dynamic-slice_convert_fusion), channel_id=1, source_target_pairs={{0,1},{1,0},{2,3},{3,2},{4,5},{5,4},{6,7},{7,6},{8,9},{9,8},{10,11... | collective-permute-start | bytes 997640 | tf_op jit(solution)/shard_map/ppermute | solution.py:317
  49.6 0.7 %copy.22 = bf16[8,2,16,384]{3,2,1,0:T(8,128)(2,1)} copy(bf16[8,2,16,384]{3,0,1,2:T(8,128)(2,1)S(1)} %bitcast.44) | data formatting | bytes 393216 | tf_op jit(solution)/shard_map/transpose | solution.py:320
  50.3 0.7 %collective-permute-done = bf16[192,866]{0,1:T(8,128)(2,1)S(1)} collective-permute-done((bf16[192,866]{0,1:T(8,128)(2,1)S(1)}, bf16[192,866]{0,1:T(8,128)(2,1)S(1)}, u32[]{:S(2)}, u32[]{:S(2)}) %collective-permute-start) | collective-permute-done | bytes 332576 | tf_op jit(solution)/shard_map/ppermute | solution.py:317
  51.0 0.3 convert_add_fusion
  51.3 0.1 slice_bitcast_fusion.1
  51.4 0.1 maximum_bitcast_fusion
  51.5 1.1 %copy.25 = f32[2,384,192]{1,2,0:T(8,128)} copy(f32[2,384,192]{2,1,0:T(8,128)S(1)} %maximum_bitcast_fusion) | data formatting | bytes 1179648
  52.6 0.7 %copy.26 = f32[2,49,192]{2,0,1:T(2,128)} copy(f32[2,49,192]{2,1,0:T(8,128)S(1)} %reshape.43) | data formatting | bytes 150528
  (6 shorter events, 0.1 us)
Async XLA Ops:
  0.6 1.4 %copy-start.2 = (bf16[1,1,8,32,384]{4,3,2,1,0:T(8,128)(2,1)S(1)}, bf16[1,1,8,32,384]{4,3,2,1,0:T(8,128)(2,1)}, u32[]{:S(2)}) copy-start(bf16[1,1,8,32,384]{4,3,2,1,0:T(8,128)(2,1)} %param.5) | copy-start | bytes 589828
  0.6 1.5 %copy-start.3 = (f32[2,49,384]{2,0,1:T(2,128)S(1)}, f32[2,49,384]{2,0,1:T(2,128)}, u32[]{:S(2)}) copy-start(f32[2,49,384]{2,0,1:T(2,128)} %param.8) | copy-start | bytes 451588
  2.2 2.5 %copy-start = (bf16[2,3,3,384,384]{4,3,2,1,0:T(8,128)(2,1)S(1)}, bf16[2,3,3,384,384]{4,3,2,1,0:T(8,128)(2,1)}, u32[]{:S(2)}) copy-start(bf16[2,3,3,384,384]{4,3,2,1,0:T(8,128)(2,1)} %param.7) | copy-start | bytes 15925252
  4.7 2.4 %copy-start.1 = (bf16[2,384,384]{2,1,0:T(8,128)(2,1)S(1)}, bf16[2,384,384]{2,1,0:T(8,128)(2,1)}, u32[]{:S(2)}) copy-start(bf16[2,384,384]{2,1,0:T(8,128)(2,1)} %point_ref.7) | copy-start | bytes 1769476
  4.7 11.1 %slice-start = ((s8[5308416]{0:T(1024)(128)(4,1)}), s8[4194304]{0:T(1024)(128)(4,1)S(1)}, s32[]{:S(2)}) async-start(s8[5308416]{0:T(1024)(128)(4,1)} %bitcast.34), calls=%async_computation | async-start | bytes 8388608
  7.1 8.7 %slice-start.1 = ((s8[5308416]{0:T(1024)(128)(4,1)}), s8[1114112]{0:T(1024)(128)(4,1)S(1)}, s32[]{:S(2)}) async-start(s8[5308416]{0:T(1024)(128)(4,1)} %bitcast.34), calls=%async_computation.1 | async-start | bytes 2228224
  48.2 2.8 %collective-permute-start = (bf16[192,866]{0,1:T(8,128)(2,1)S(1)}, bf16[192,866]{0,1:T(8,128)(2,1)S(1)}, u32[]{:S(2)}, u32[]{:S(2)}) collective-permute-start(bf16[192,866]{0,1:T(8,128)(2,1)S(1)} %dynamic-slice_convert_fusion), channel_id=1, source_target_pairs={{0,1},{1,0},{2,3},{3,2},{4,5},{5,4},{6,7},{7,6},{8,9},{9,8},{10,11... | collective-permute-start | bytes 997640 | tf_op jit(solution)/shard_map/ppermute | solution.py:317
where the time goes:
time: 53.4 us; the launch traced here: 53.2 us
  Pallas kernels  41.7 us (78%)
  local copies, waits for them, and re-layouts  6.82 us (13%)
  starting transfers between devices  1.35 us (3%)
  matrix products  1.24 us (2%)
  between operations  0.87 us (2%)
  waiting for transfers between devices  0.71 us (1%)
    pallas_call x4, Pallas kernels, student(): pl.pallas_call(functools.partial(student_kernel, height, half // 2, secti...  32.4 us
    pallas_call x4, Pallas kernels, teacher(): pl.pallas_call(functools.partial(teacher_kernel, height), out_shape=(jax....  9.31 us
    unnamed x17, local copies, waits for them, and re-layouts  4.35 us
    another operation x2, local copies, waits for them, and re-layouts, to_rows(): split = maps.reshape(front + (height, 2, width // 2, chans))  1.37 us
    ppermute x1, starting transfers between devices, body(): total = total + lax.ppermute(out.astype(BF16), 'dp', pairs).astype(F32)  1.35 us
    dot_general x2, matrix products, body(): lax.dot_general(grad_all[b], gel_all[b], (((0,), (0,)), ((), ())), prefer...  1.24 us
  transfers between devices with their start and end apart: 1, of which 1 were waited for; matrix products, arithmetic and copies ran while one was open for 1% of the time, Pallas kernels for 0%

commit v1 on v0

v1 whole, which is shorter than its diff:
```python
import functools

import jax
import jax.numpy as jnp
from jax import lax
from jax.experimental import pallas as pl
from jax.experimental.pallas import tpu as pltpu
from jax.sharding import PartitionSpec as P

LANES = 128
F32 = jnp.float32
BF16 = jnp.bfloat16
MESH = pl.DeviceIdType.MESH
NT = (((1,), (1,)), ((), ()))


def lanes(block):
    return slice(block * LANES, (block + 1) * LANES)


def columns(block):
    return pl.ds(pl.multiple_of(block * LANES, LANES), LANES)


def put_padded(vals, pad_ref, height):
    units = vals.shape[0] // (2 * height)
    for block in range(vals.shape[1] // LANES):
        for unit in range(units):
            for half in range(2):
                at = (2 * unit + half) * height
                to = (2 * (unit + half * units) + 1) * height
                pad_ref[block, to : to + height] = vals[at : at + height, lanes(block)]


def spread(pad_ref, out_ref, height, units, reach):
    blocks, taps = out_ref.shape[0], 2 * reach + 1

    def one_row(row, carry):
        for block in range(blocks):

            def load(w):
                return pad_ref[block, pl.ds((2 * w + 1) * height + row - reach, height)]

            zero = jnp.zeros((height, LANES), F32)
            cols = [load(w) for w in range(2 * units)]
            low = [zero] * reach + cols[: units + reach]
            high = cols[units - reach :] + [zero] * reach
            for unit in range(units + 2 * reach):
                out_ref[block, row, unit] = jnp.concatenate([low[unit], high[unit]], axis=0).astype(BF16)
        return carry

    lax.fori_loop(0, taps, one_row, 0)


def tap_sum(src_ref, block, coef_ref, which, start, count, flip):
    total = None
    for rows in ((0, 1, 2, 3), (4, 5, 6)):
        part = None
        for row in rows:
            strip = src_ref[block, row, pl.ds(start, count + 6)]
            acc = None
            for col in range(7):
                tap = row * 7 + col
                tap = 48 - tap if flip else tap
                term = strip[col : col + count] * coef_ref[which, block, tap][None]
                acc = term if acc is None else acc + term
            part = acc if part is None else part + acc
        wide = part.astype(F32)
        total = wide if total is None else total + wide
    return total


def gelu_pair(act):
    root = 0.7978845608028654
    cubic = root * 0.044715
    square = act * act
    tanh = jnp.tanh(act * (root + cubic * square))
    half = 0.5 + 0.5 * tanh
    slope = half + (half - half * half) * (act * (2.0 * root + 6.0 * cubic * square))
    return act * half, slope


def tick_kernel(height, step, sections, first, lead_ref, fresh_ref, relay_ref, weight_ref, coef_ref, point_ref, *rest):
    if not first:
        prev_ref, *rest = rest
    teach_ref, gel0, gel1, grad0, grad1, dk_ref, *rest = rest
    if sections:
        next_ref, *rest = rest
        *rest, land, send_sem, recv_sem = rest
        spot = lax.axis_index("section")
        later, earlier = lax.rem(spot + 1, sections), lax.rem(spot + sections - 1, sections)
        barrier = pltpu.get_barrier_semaphore()

        @pl.when(spot > 0)
        def _():
            pl.semaphore_signal(barrier, inc=1, device_id={"section": earlier}, device_id_type=MESH)

        copy = pltpu.make_async_remote_copy(
            src_ref=teach_ref,
            dst_ref=land,
            send_sem=send_sem,
            recv_sem=recv_sem,
            device_id={"section": later},
            device_id_type=MESH,
        )
    pad, hpad, src0, src1, src2, hid, slope0, slope1, dact0, cur_ref, u_one_ref, resid_ref, acc1, acc2 = rest
    gels, grads = (gel0, gel1), (grad0, grad1)
    srcs, slopes = (src0, src1), (slope0, slope1)
    rows, chans = cur_ref.shape
    blocks = chans // LANES
    pair = 2 * height
    units = rows // pair
    chunks = units // step
    pads = pad.shape[1]

    def span(index):
        return pl.ds(pl.multiple_of(index * step * pair, step * pair), step * pair)

    zero = jnp.zeros((height, LANES), F32)
    for block in range(blocks):
        for at in range(0, pads, pair):
            pad[block, at : at + height] = zero
            hpad[block, at : at + height] = zero

    lead = lead_ref[0] == 1
    current = jnp.where(lead, fresh_ref[...].astype(F32), relay_ref[...].astype(F32))
    cur_ref[...] = current
    put_padded(current, pad, height)
    spread(pad, src0, height, units, 3)
    acc1[...] = jnp.zeros_like(acc1)
    acc2[...] = jnp.zeros_like(acc2)

    def teach_chunk(at, src_ref, middle, which, acc):
        down, index = at // chunks, lax.rem(at, chunks)
        parts = []
        for right in range(3):
            start = index * step + middle - 1 + right
            for block in range(blocks):
                part = src_ref[block, middle - 1 + down, pl.ds(start, step)]
                parts.append(part.reshape(step * pair, LANES))
        deep = 3 * chans
        weights = weight_ref[which, pl.ds(pl.multiple_of(down * deep, deep), deep)]
        acc[span(index)] += jnp.dot(jnp.concatenate(parts, axis=1), weights, preferred_element_type=F32)

    def forward(which, src_ref, middle, acc):
        def chunk(at, carry):
            block, index = at // chunks, lax.rem(at, chunks)
            act = tap_sum(srcs[which], block, coef_ref, which, index * step, step, False)
            teach_chunk(at, src_ref, middle, which, acc)
            gel, slope = gelu_pair(act.reshape(step * pair, LANES))
            slopes[which][span(index), columns(block)] = slope
            gels[which][span(index), columns(block)] = gel.astype(BF16)
            return carry

        lax.fori_loop(0, blocks * chunks, chunk, 0)
        return jnp.dot(gels[which][...], point_ref[which], preferred_element_type=F32)

    u_one = forward(0, src0, 3, acc1) + cur_ref[...]
    u_one_ref[...] = u_one
    put_padded(u_one, pad, height)
    put_padded(jnp.maximum(acc1[...], 0.0), hpad, height)
    spread(hpad, hid, height, units, 1)
    spread(pad, src1, height, units, 3)

    diff = forward(1, hid, 1, acc2) + u_one_ref[...]
    teach = (0.8 * (cur_ref[...] + acc2[...])).astype(BF16)
    teach_ref[...] = teach
    resid = (diff - teach.astype(F32)) * (4.0 / rows)
    resid_ref[...] = resid
    grad1[...] = resid.astype(BF16)

    def back_point(which):
        dgel = lax.dot_general(grads[which][...], point_ref[which], NT, preferred_element_type=F32)
        return dgel * slopes[which][...]

    put_padded(back_point(1), pad, height)
    if sections:

        @pl.when(spot < sections - 1)
        def _():
            pl.semaphore_wait(barrier, 1)
            copy.start()

    spread(pad, src2, height, units, 3)

    def chunk_back(at, carry):
        block, index = at // chunks, lax.rem(at, chunks)
        back = tap_sum(src2, block, coef_ref, 1, index * step, step, True)
        back = back.reshape(step * pair, LANES) + resid_ref[span(index), columns(block)]
        grad0[span(index), columns(block)] = back.astype(BF16)
        return carry

    lax.fori_loop(0, blocks * chunks, chunk_back, 0)

    def taps_grad(which, part_of):
        def over_rows(row, carry):
            for block in range(blocks):
                strip = srcs[which][block, row]
                part = part_of(block)
                for col in range(7):
                    prod = strip[col : col + units] * part
                    size = units
                    while size > 1:
                        size //= 2
                        prod = prod[:size] + prod[size:]
                    wide = prod[0].astype(F32)
                    total = wide[:height] + wide[height:]
                    if not first:
                        total = total + prev_ref[which, block, row, col]
                    dk_ref[which, block, row, col] = total
            return carry

        lax.fori_loop(0, 7, over_rows, 0)

    taps_grad(1, lambda block: src2[block, 3, 3 : 3 + units])
    dact = back_point(0)
    for block in range(blocks):
        dact0[block] = dact[:, lanes(block)].reshape(units, pair, LANES).astype(BF16)
    taps_grad(0, lambda block: dact0[block])
    if sections:

        @pl.when(spot > 0)
        def _():
            copy.wait_recv()
            next_ref[...] = land[...]

        @pl.when(spot == 0)
        def _():
            next_ref[...] = jnp.zeros_like(next_ref)

        @pl.when(spot < sections - 1)
        def _():
            copy.wait_send()


def tick_call(lead, fresh, relay, weight, coef, point, prev, height, sections):
    rows, chans = fresh.shape
    blocks = chans // LANES
    pair = 2 * height
    units = rows // pair
    vmem = pl.BlockSpec(memory_space=pltpu.VMEM)
    flat = jax.ShapeDtypeStruct((rows, chans), BF16)
    outs = [flat] * 5 + [jax.ShapeDtypeStruct((2, blocks, 7, 7, height, LANES), F32)]
    pad_shape = pltpu.VMEM((blocks, (2 * 2 * units + 1) * height, LANES), F32)
    src_shape = pltpu.VMEM((blocks, 7, units + 6, pair, LANES), BF16)
    map_shape = pltpu.VMEM((rows, chans), F32)
    scratch = [pad_shape] * 2 + [src_shape] * 3
    scratch += [pltpu.VMEM((blocks, 3, units + 2, pair, LANES), BF16)]
    scratch += [map_shape] * 2 + [pltpu.VMEM((blocks, units, pair, LANES), BF16)] + [map_shape] * 5
    params = {}
    if sections:
        outs.append(flat)
        scratch += [pltpu.VMEM((rows, chans), BF16), pltpu.SemaphoreType.DMA, pltpu.SemaphoreType.DMA]
        params = {"collective_id": 0 if prev is None else 1, "has_side_effects": True}
    args = [lead, fresh, relay, weight, coef, point] + ([] if prev is None else [prev])
    return pl.pallas_call(
        functools.partial(tick_kernel, height, units // 2, sections, prev is None),
        out_shape=tuple(outs),
        in_specs=[pl.BlockSpec(memory_space=pltpu.SMEM)] + [vmem] * (len(args) - 1),
        out_specs=(vmem,) * len(outs),
        scratch_shapes=scratch,
        compiler_params=pltpu.CompilerParams(vmem_limit_bytes=24 << 20, **params),
        cost_estimate=pl.CostEstimate(
            flops=10_000_000_000, bytes_accessed=8 * rows * chans, transcendentals=0
        ),
        name="tick",
    )(*args)


def body(pipe_maps, fresh_maps, teacher_weight, student_depth, student_point):
    _, _, height, width, chans = pipe_maps.shape
    rows = height * width
    blocks = chans // LANES
    lead = (lax.axis_index("section") == 0).astype(jnp.int32).reshape(1)
    sections = lax.axis_size("section")

    def to_rows(maps):
        front = maps.shape[:-3]
        split = maps.reshape(front + (height, 2, width // 2, chans))
        return jnp.swapaxes(split, -4, -2).reshape(front + (rows, chans))

    relay = to_rows(pipe_maps[0, 0])
    fresh = to_rows(fresh_maps[:, 0])
    weight = teacher_weight.reshape(2, 9 * chans, chans)
    coef = student_depth.astype(BF16).reshape(2, 49, blocks, 1, LANES).swapaxes(1, 2)
    coef = jnp.broadcast_to(coef, (2, blocks, 49, 2 * height, LANES))
    ticks = fresh_maps.shape[0] + 1
    gels, grads, depth_total = [], [], None
    teach = relay
    for tick in range(ticks):
        mine = relay if tick == 0 else fresh[tick - 1]
        linked = sections if tick + 1 < ticks else 0
        teach, gel0, gel1, grad0, grad1, depth_total, *sent = tick_call(
            lead, mine, relay, weight, coef, student_point, depth_total, height, linked
        )
        if sent:
            relay = sent[0]
        gels.append((gel0, gel1))
        grads.append((grad0, grad1))
    gel_all = [jnp.concatenate([pair[b] for pair in gels]) for b in range(2)]
    grad_all = [jnp.concatenate([pair[b] for pair in grads]) for b in range(2)]
    point_total = [
        lax.dot_general(grad_all[b], gel_all[b], (((0,), (0,)), ((), ())), preferred_element_type=F32)
        for b in range(2)
    ]
    depth_rows = depth_total.sum(axis=4).transpose(1, 4, 0, 2, 3).reshape(chans, 98)
    packed = jnp.concatenate(point_total + [depth_rows], axis=1)
    parties = lax.axis_size("dp")
    share = chans // parties
    me = lax.axis_index("dp")
    total = lax.dynamic_slice_in_dim(packed, me * share, share, 0)
    for hop in range(1, parties):
        out = lax.dynamic_slice_in_dim(packed, lax.rem(me + hop, parties) * share, share, 0)
        pairs = [(i, (i + hop) % parties) for i in range(parties)]
        total = total + lax.ppermute(out.astype(BF16), "dp", pairs).astype(F32)
    point_grad = jnp.stack([total[:, b * chans : (b + 1) * chans] for b in range(2)]).swapaxes(1, 2)
    depth_grad = total[:, 2 * chans :].T.reshape(2, 49, share)
    final = jnp.swapaxes(teach.reshape(width // 2, 2, height, chans), 0, 2)
    final = final.reshape(1, 1, height, width, chans)
    return final, point_grad, depth_grad


def solution(mesh):
    placed = (
        P("section", "dp", None, None, None),
        P(None, "dp", None, None, None),
        P("section", None, None, None, None),
        P("section", None, None),
        P("section", None, None),
    )
    return jax.shard_map(
        body,
        mesh=mesh,
        in_specs=placed,
        out_specs=(
            P("section", "dp", None, None, None),
            P("section", None, "dp"),
            P("section", None, "dp"),
        ),
        check_vma=False,
    )
```

time: 53.4 us -> 75.7 us (1.42)
  Pallas kernels: 41.7 us -> 57.5 us
  local copies, waits for them, and re-layouts: 6.82 us -> 10.8 us
  matrix products: 1.24 us -> 2.5 us
  other arithmetic: 0.51 us -> 1.72 us
    pallas_call x8 -> x4, Pallas kernels: 41.7 us -> 57.5 us  [tick_call(): pl.pallas_call(functools.partial(tick_kernel, height, units // 2, section...]
    unnamed x17 -> x24, local copies, waits for them, and re-layouts: 4.35 us -> 7.04 us
    dot_general x2, matrix products: 1.24 us -> 2.5 us  [body(): lax.dot_general(grad_all[b], gel_all[b], (((0,), (0,)), ((), ())), prefer...]
    convert_element_type x0 -> x1, other arithmetic: none -> 0.96 us  [body(): student_depth.astype(BF16).reshape(2, 49, blocks, 1, LANES).swapaxes(1, 2)]
    another operation x2, local copies, waits for them, and re-layouts: 1.37 us -> 2.32 us  [to_rows(): split = maps.reshape(front + (height, 2, width // 2, chans))]
where the time goes in v1:
time: 75.7 us; the launch traced here: 75.4 us
  Pallas kernels  57.5 us (76%)
  local copies, waits for them, and re-layouts  10.8 us (14%)
  matrix products  2.5 us (3%)
  other arithmetic  1.72 us (2%)
  starting transfers between devices  1.32 us (2%)
  between operations  0.91 us (1%)
    pallas_call x4, Pallas kernels, tick_call(): pl.pallas_call(functools.partial(tick_kernel, height, units // 2, section...  57.5 us
    unnamed x24, local copies, waits for them, and re-layouts  7.04 us
    dot_general x2, matrix products, body(): lax.dot_general(grad_all[b], gel_all[b], (((0,), (0,)), ((), ())), prefer...  2.5 us
    another operation x2, local copies, waits for them, and re-layouts, to_rows(): split = maps.reshape(front + (height, 2, width // 2, chans))  2.32 us
  transfers between devices with their start and end apart: 1, of which 1 were waited for; matrix products, arithmetic and copies ran while one was open for 1% of the time, Pallas kernels for 0%

profile of v1, /device:TPU:25, one launch (start us, length us, event | category | flops | bytes accessed | tf_op | source)
XLA Modules:
  0.0 75.4 jit_solution(16233249290008972083)
XLA Ops:
  0.6 1.0 %convert_element_type.10 = bf16[2,49,384]{2,0,1:T(2,128)(2,1)S(1)} convert(f32[2,49,384]{2,0,1:T(2,128)} %param.8) | non-fusion elementwise | flops 37632 | bytes 225792 | tf_op jit(solution)/shard_map/convert_element_type | solution.py:285
  1.6 0.1 reshape.43
  1.8 1.0 %copy.21 = bf16[8,2,16,384]{3,0,1,2:T(8,128)(2,1)S(1)} copy(bf16[8,2,16,384]{3,2,1,0:T(8,128)(2,1)} %bitcast.54) | data formatting | bytes 393216 | tf_op jit(solution)/shard_map/reshape;squeeze | solution.py:279
  2.8 0.0 copy-start.1
  2.8 1.3 %copy.29 = bf16[3,8,2,16,384]{4,1,2,3,0:T(8,128)(2,1)S(1)} copy(bf16[3,8,2,16,384]{4,3,2,1,0:T(8,128)(2,1)} %bitcast.52) | data formatting | bytes 1179648 | tf_op jit(solution)/shard_map/reshape;squeeze | solution.py:279
  4.1 0.1 fusion.32
  4.2 0.2 broadcast_in_dim.8.coef_ref
  4.3 0.0 copy-done.1
  4.3 0.0 copy-start
  4.4 2.5 %copy-done = bf16[2,3,3,384,384]{4,3,2,1,0:T(8,128)(2,1)S(1)} copy-done((bf16[2,3,3,384,384]{4,3,2,1,0:T(8,128)(2,1)S(1)}, bf16[2,3,3,384,384]{4,3,2,1,0:T(8,128)(2,1)}, u32[]{:S(2)}) %copy-start) | copy-done | bytes 5308440
  6.9 15.1 %tick.4 = (bf16[256,384]{1,0:T(8,128)(2,1)}, bf16[256,384]{1,0:T(8,128)(2,1)S(1)}, bf16[256,384]{1,0:T(8,128)(2,1)S(1)}, bf16[256,384]{1,0:T(8,128)(2,1)S(1)}, b...) custom-call(s32[1]{0:T(128)} %bitcast.lead_ref, ...), custom_call_target="tpu_custom_call" | custom-call | flops 10000000000 | bytes 786432 | tf_op jit(solution)/shard_map/tick/pallas_call | solution.py:256
  22.0 14.3 %tick.5 = (bf16[256,384]{1,0:T(8,128)(2,1)}, bf16[256,384]{1,0:T(8,128)(2,1)S(1)}, bf16[256,384]{1,0:T(8,128)(2,1)S(1)}, bf16[256,384]{1,0:T(8,128)(2,1)S(1)}, b...) custom-call(s32[1]{0:T(128)} %bitcast.lead_ref, ...), custom_call_target="tpu_custom_call" | custom-call | flops 10000000000 | bytes 786432 | tf_op jit(solution)/shard_map/tick/pallas_call | solution.py:256
  36.3 14.5 %tick.6 = (bf16[256,384]{1,0:T(8,128)(2,1)}, bf16[256,384]{1,0:T(8,128)(2,1)S(1)}, bf16[256,384]{1,0:T(8,128)(2,1)S(1)}, bf16[256,384]{1,0:T(8,128)(2,1)S(1)}, b...) custom-call(s32[1]{0:T(128)} %bitcast.lead_ref, ...), custom_call_target="tpu_custom_call" | custom-call | flops 10000000000 | bytes 786432 | tf_op jit(solution)/shard_map/tick/pallas_call | solution.py:256
  50.8 0.0 copy-start.6
  50.8 0.0 copy-start.7
  50.8 13.6 %tick.7 = (bf16[256,384]{1,0:T(8,128)(2,1)S(1)}, bf16[256,384]{1,0:T(8,128)(2,1)S(1)}, bf16[256,384]{1,0:T(8,128)(2,1)S(1)}, bf16[256,384]{1,0:T(8,128)(2,1)S(1)...) custom-call(s32[1]{0:T(128)} %bitcast.lead_ref, bf16[256,384]{1,0:T(8,128)(2,1)S(1)} %bitcast.37, ...), custom_call_target="tpu_custom_call" | custom-call | flops 10000000000 | bytes 786432 | tf_op jit(solution)/shard_map/tick/pallas_call | solution.py:256
  64.4 0.0 copy-done.6
  64.4 0.0 copy-done.7
  64.4 0.0 copy-start.2
  64.4 0.7 copy-done.2
  65.1 0.0 copy-start.4
  65.1 0.7 copy-done.4
  65.8 0.0 copy-start.8
  65.8 0.7 copy-done.8
  66.5 0.0 copy-start.9
  66.5 0.7 copy-done.9
  67.1 0.3 reduce_sum.9
  67.4 0.1 copy.24
  67.6 0.0 copy-start.3
  67.6 0.0 copy-start.5
  67.6 1.9 %fusion = f32[384,384]{0,1:T(8,128)S(1)} fusion(bf16[256,384]{1,0:T(8,128)(2,1)} %copy-done.9, bf16[256,384]{1,0:T(8,128)(2,1)} %copy-done.7, bf16[256,384]{1,0:T(8,128)(2,1)S(1)} %get-tuple-element.35, bf16[256,384]{1,0:T(8,128)(2,1)S(1)} %get-tuple-element.34, bf16[256,384]{1,0:T(8,128)(2,1)} %copy-done.8, bf16[256,384]{1,0:T(8,128)(2,1)} %copy-done.6, ...), kind=kOutput, calls=%fused_computation.3 | convolution fusion | flops 308281344 | bytes 2162688 | tf_op jit(solution)/shard_map/dot_general | solution.py:303
  69.5 0.0 copy-done.3
  69.5 0.0 copy-done.5
  69.5 0.6 fusion.15
  70.1 0.1 pad_maximum_fusion
  70.2 0.2 dynamic-slice_convert_fusion
  70.4 1.3 %collective-permute-start = (bf16[192,866]{0,1:T(8,128)(2,1)S(1)}, bf16[192,866]{0,1:T(8,128)(2,1)S(1)}, u32[]{:S(2)}, u32[]{:S(2)}) collective-permute-start(bf16[192,866]{0,1:T(8,128)(2,1)S(1)} %dynamic-slice_convert_fusion), channel_id=1, source_target_pairs={{0,1},{1,0},{2,3},{3,2},{4,5},{5,4},{6,7},{7,6},{8,9},{9,8},{10,11... | collective-permute-start | bytes 997640 | tf_op jit(solution)/shard_map/ppermute | solution.py:315
  71.8 0.7 copy.23
  72.5 0.7 collective-permute-done
  73.2 0.3 convert_add_fusion
  73.5 0.1 slice_bitcast_fusion.1
  73.6 0.1 maximum_bitcast_fusion
  73.6 1.1 %copy.25 = f32[2,384,192]{1,2,0:T(8,128)} copy(f32[2,384,192]{2,1,0:T(8,128)S(1)} %maximum_bitcast_fusion) | data formatting | bytes 1179648
  74.7 0.7 copy.26
  (5 shorter events, 0.1 us)
Async XLA Ops:
  2.8 1.6 %copy-start.1 = (bf16[2,384,384]{2,1,0:T(8,128)(2,1)S(1)}, bf16[2,384,384]{2,1,0:T(8,128)(2,1)}, u32[]{:S(2)}) copy-start(bf16[2,384,384]{2,1,0:T(8,128)(2,1)} %point_ref.7) | copy-start | bytes 1769476
  4.3 2.5 %copy-start = (bf16[2,3,3,384,384]{4,3,2,1,0:T(8,128)(2,1)S(1)}, bf16[2,3,3,384,384]{4,3,2,1,0:T(8,128)(2,1)}, u32[]{:S(2)}) copy-start(bf16[2,3,3,384,384]{4,3,2,1,0:T(8,128)(2,1)} %param.7) | copy-start | bytes 15925252
  50.8 13.6 %copy-start.6 = (bf16[256,384]{1,0:T(8,128)(2,1)}, bf16[256,384]{1,0:T(8,128)(2,1)S(1)}, u32[]{:S(2)}) copy-start(bf16[256,384]{1,0:T(8,128)(2,1)S(1)} %get-tuple-element.40) | copy-start | bytes 589828
  50.8 13.6 %copy-start.7 = (bf16[256,384]{1,0:T(8,128)(2,1)}, bf16[256,384]{1,0:T(8,128)(2,1)S(1)}, u32[]{:S(2)}) copy-start(bf16[256,384]{1,0:T(8,128)(2,1)S(1)} %get-tuple-element.36) | copy-start | bytes 589828
  64.4 0.7 copy-start.2
  65.1 0.7 copy-start.4
  65.8 0.7 copy-start.8
  66.5 0.7 copy-start.9
  67.6 1.9 %copy-start.3 = (bf16[256,384]{1,0:T(8,128)(2,1)S(1)}, bf16[256,384]{1,0:T(8,128)(2,1)}, u32[]{:S(2)}) copy-start(bf16[256,384]{1,0:T(8,128)(2,1)} %copy-done.2) | copy-start | bytes 589828
  67.6 1.9 %copy-start.5 = (bf16[256,384]{1,0:T(8,128)(2,1)S(1)}, bf16[256,384]{1,0:T(8,128)(2,1)}, u32[]{:S(2)}) copy-start(bf16[256,384]{1,0:T(8,128)(2,1)} %copy-done.4) | copy-start | bytes 589828
  70.4 2.7 %collective-permute-start = (bf16[192,866]{0,1:T(8,128)(2,1)S(1)}, bf16[192,866]{0,1:T(8,128)(2,1)S(1)}, u32[]{:S(2)}, u32[]{:S(2)}) collective-permute-start(bf16[192,866]{0,1:T(8,128)(2,1)S(1)} %dynamic-slice_convert_fusion), channel_id=1, source_target_pairs={{0,1},{1,0},{2,3},{3,2},{4,5},{5,4},{6,7},{7,6},{8,9},{9,8},{10,11... | collective-permute-start | bytes 997640 | tf_op jit(solution)/shard_map/ppermute | solution.py:315

commit v2 on v1

--- a/solution.py
+++ b/solution.py
@@ -32,11 +32,9 @@
                 pad_ref[block, to : to + height] = vals[at : at + height, lanes(block)]
 
 
-def spread(pad_ref, out_ref, height, units, reach):
-    blocks, taps = out_ref.shape[0], 2 * reach + 1
-
+def spread(pad_ref, put, height, units, reach):
     def one_row(row, carry):
-        for block in range(blocks):
+        for block in range(pad_ref.shape[0]):
 
             def load(w):
                 return pad_ref[block, pl.ds((2 * w + 1) * height + row - reach, height)]
@@ -46,10 +44,34 @@
             low = [zero] * reach + cols[: units + reach]
             high = cols[units - reach :] + [zero] * reach
             for unit in range(units + 2 * reach):
-                out_ref[block, row, unit] = jnp.concatenate([low[unit], high[unit]], axis=0).astype(BF16)
+                put(block, row, unit, low[unit], high[unit])
         return carry
 
-    lax.fori_loop(0, taps, one_row, 0)
+    lax.fori_loop(0, 2 * reach + 1, one_row, 0)
+
+
+def strips(out_ref):
+    def put(block, row, unit, low, high):
+        out_ref[block, row, unit] = jnp.concatenate([low, high], axis=1).astype(BF16)
+
+    return put
+
+
+def windows(out_ref, height):
+    def put(block, row, unit, low, high):
+        at = slice(unit * 2 * height, (unit + 1) * 2 * height)
+        out_ref[row, at, lanes(block)] = jnp.concatenate([low, high], axis=0).astype(BF16)
+
+    return put
+
+
+def beside(vals, height):
+    split = vals.reshape(-1, 2 * height, LANES)
+    return jnp.concatenate([split[:, :height], split[:, height:]], axis=2)
+
+
+def below(vals, height):
+    return jnp.concatenate([vals[:, :, :LANES], vals[:, :, LANES:]], axis=1).reshape(-1, LANES)
 
 
 def tap_sum(src_ref, block, coef_ref, which, start, count, flip):
@@ -103,7 +125,7 @@
             device_id={"section": later},
             device_id_type=MESH,
         )
-    pad, hpad, src0, src1, src2, hid, slope0, slope1, dact0, cur_ref, u_one_ref, resid_ref, acc1, acc2 = rest
+    pad, hpad, src0, src1, src2, win, slope0, slope1, dact0, cur_ref, u_one_ref, resid_ref, acc1, acc2 = rest
     gels, grads = (gel0, gel1), (grad0, grad1)
     srcs, slopes = (src0, src1), (slope0, slope1)
     rows, chans = cur_ref.shape
@@ -126,43 +148,42 @@
     current = jnp.where(lead, fresh_ref[...].astype(F32), relay_ref[...].astype(F32))
     cur_ref[...] = current
     put_padded(current, pad, height)
-    spread(pad, src0, height, units, 3)
+    spread(pad, windows(win, height), height, units, 1)
+    spread(pad, strips(src0), height, units, 3)
     acc1[...] = jnp.zeros_like(acc1)
     acc2[...] = jnp.zeros_like(acc2)
 
-    def teach_chunk(at, src_ref, middle, which, acc):
+    def teach_chunk(at, which, acc):
         down, index = at // chunks, lax.rem(at, chunks)
         parts = []
         for right in range(3):
-            start = index * step + middle - 1 + right
-            for block in range(blocks):
-                part = src_ref[block, middle - 1 + down, pl.ds(start, step)]
-                parts.append(part.reshape(step * pair, LANES))
+            start = pl.multiple_of((index * step + right) * pair, pair)
+            parts.append(win[down, pl.ds(start, step * pair)])
         deep = 3 * chans
         weights = weight_ref[which, pl.ds(pl.multiple_of(down * deep, deep), deep)]
         acc[span(index)] += jnp.dot(jnp.concatenate(parts, axis=1), weights, preferred_element_type=F32)
 
-    def forward(which, src_ref, middle, acc):
+    def forward(which, acc):
         def chunk(at, carry):
             block, index = at // chunks, lax.rem(at, chunks)
             act = tap_sum(srcs[which], block, coef_ref, which, index * step, step, False)
-            teach_chunk(at, src_ref, middle, which, acc)
-            gel, slope = gelu_pair(act.reshape(step * pair, LANES))
+            teach_chunk(at, which, acc)
+            gel, slope = gelu_pair(below(act, height))
             slopes[which][span(index), columns(block)] = slope
             gels[which][span(index), columns(block)] = gel.astype(BF16)
             return carry
 
-        lax.fori_loop(0, blocks * chunks, chunk, 0)
+        lax.fori_loop(0, blocks * chunks, chunk, 0, unroll=blocks)
         return jnp.dot(gels[which][...], point_ref[which], preferred_element_type=F32)
 
-    u_one = forward(0, src0, 3, acc1) + cur_ref[...]
+    u_one = forward(0, acc1) + cur_ref[...]
     u_one_ref[...] = u_one
     put_padded(u_one, pad, height)
     put_padded(jnp.maximum(acc1[...], 0.0), hpad, height)
-    spread(hpad, hid, height, units, 1)
-    spread(pad, src1, height, units, 3)
-
-    diff = forward(1, hid, 1, acc2) + u_one_ref[...]
+    spread(hpad, windows(win, height), height, units, 1)
+    spread(pad, strips(src1), height, units, 3)
+
+    diff = forward(1, acc2) + u_one_ref[...]
     teach = (0.8 * (cur_ref[...] + acc2[...])).astype(BF16)
     teach_ref[...] = teach
     resid = (diff - teach.astype(F32)) * (4.0 / rows)
@@ -181,20 +202,21 @@
             pl.semaphore_wait(barrier, 1)
             copy.start()
 
-    spread(pad, src2, height, units, 3)
+    spread(pad, strips(src2), height, units, 3)
 
     def chunk_back(at, carry):
         block, index = at // chunks, lax.rem(at, chunks)
         back = tap_sum(src2, block, coef_ref, 1, index * step, step, True)
-        back = back.reshape(step * pair, LANES) + resid_ref[span(index), columns(block)]
+        back = below(back, height) + resid_ref[span(index), columns(block)]
         grad0[span(index), columns(block)] = back.astype(BF16)
         return carry
 
     lax.fori_loop(0, blocks * chunks, chunk_back, 0)
 
     def taps_grad(which, part_of):
-        def over_rows(row, carry):
-            for block in range(blocks):
+        for block in range(blocks):
+
+            def over_rows(row, carry):
                 strip = srcs[which][block, row]
                 part = part_of(block)
                 for col in range(7):
@@ -204,18 +226,18 @@
                         size //= 2
                         prod = prod[:size] + prod[size:]
                     wide = prod[0].astype(F32)
-                    total = wide[:height] + wide[height:]
+                    total = wide[:, :LANES] + wide[:, LANES:]
                     if not first:
                         total = total + prev_ref[which, block, row, col]
                     dk_ref[which, block, row, col] = total
-            return carry
-
-        lax.fori_loop(0, 7, over_rows, 0)
+                return carry
+
+            lax.fori_loop(0, 7, over_rows, 0)
 
     taps_grad(1, lambda block: src2[block, 3, 3 : 3 + units])
     dact = back_point(0)
     for block in range(blocks):
-        dact0[block] = dact[:, lanes(block)].reshape(units, pair, LANES).astype(BF16)
+        dact0[block] = beside(dact[:, lanes(block)], height).astype(BF16)
     taps_grad(0, lambda block: dact0[block])
     if sections:
 
@@ -242,11 +264,11 @@
     flat = jax.ShapeDtypeStruct((rows, chans), BF16)
     outs = [flat] * 5 + [jax.ShapeDtypeStruct((2, blocks, 7, 7, height, LANES), F32)]
     pad_shape = pltpu.VMEM((blocks, (2 * 2 * units + 1) * height, LANES), F32)
-    src_shape = pltpu.VMEM((blocks, 7, units + 6, pair, LANES), BF16)
+    src_shape = pltpu.VMEM((blocks, 7, units + 6, height, 2 * LANES), BF16)
     map_shape = pltpu.VMEM((rows, chans), F32)
     scratch = [pad_shape] * 2 + [src_shape] * 3
-    scratch += [pltpu.VMEM((blocks, 3, units + 2, pair, LANES), BF16)]
-    scratch += [map_shape] * 2 + [pltpu.VMEM((blocks, units, pair, LANES), BF16)] + [map_shape] * 5
+    scratch += [pltpu.VMEM((3, (units + 2) * pair, chans), BF16)]
+    scratch += [map_shape] * 2 + [pltpu.VMEM((blocks, units, height, 2 * LANES), BF16)] + [map_shape] * 5
     params = {}
     if sections:
         outs.append(flat)
@@ -282,8 +304,8 @@
     relay = to_rows(pipe_maps[0, 0])
     fresh = to_rows(fresh_maps[:, 0])
     weight = teacher_weight.reshape(2, 9 * chans, chans)
-    coef = student_depth.astype(BF16).reshape(2, 49, blocks, 1, LANES).swapaxes(1, 2)
-    coef = jnp.broadcast_to(coef, (2, blocks, 49, 2 * height, LANES))
+    coef = student_depth.astype(BF16).reshape(2, 49, blocks, 1, 1, LANES).swapaxes(1, 2)
+    coef = jnp.broadcast_to(coef, (2, blocks, 49, height, 2, LANES)).reshape(2, blocks, 49, height, 2 * LANES)
     ticks = fresh_maps.shape[0] + 1
     gels, grads, depth_total = [], [], None
     teach = relay

time: 75.7 us -> 59.5 us (0.79)
  Pallas kernels: 57.5 us -> 40.7 us
  starting transfers between devices: 1.32 us -> 2.48 us
    pallas_call x4, Pallas kernels: 57.5 us -> 40.7 us  [tick_call(): pl.pallas_call(functools.partial(tick_kernel, height, units // 2, section...]
    another operation x2, local copies, waits for them, and re-layouts: 2.32 us -> 0.26 us  [to_rows(): split = maps.reshape(front + (height, 2, width // 2, chans))]
    ppermute x1, starting transfers between devices: 1.32 us -> 2.48 us  [body(): total = total + lax.ppermute(out.astype(BF16), 'dp', pairs).astype(F32)]
    unnamed x24 -> x28, local copies, waits for them, and re-layouts: 7.04 us -> 7.87 us
where the time goes in v2:
time: 59.5 us; the launch traced here: 59.2 us
  Pallas kernels  40.7 us (68%)
  local copies, waits for them, and re-layouts  10.1 us (17%)
  matrix products  2.5 us (4%)
  starting transfers between devices  2.48 us (4%)
  other arithmetic  1.79 us (3%)
  between operations  0.95 us (2%)
  waiting for transfers between devices  0.71 us (1%)
    pallas_call x4, Pallas kernels, tick_call(): pl.pallas_call(functools.partial(tick_kernel, height, units // 2, section...  40.7 us
    unnamed x28, local copies, waits for them, and re-layouts  7.87 us
    dot_general x2, matrix products, body(): lax.dot_general(grad_all[b], gel_all[b], (((0,), (0,)), ((), ())), prefer...  2.5 us
    ppermute x1, starting transfers between devices, body(): total = total + lax.ppermute(out.astype(BF16), 'dp', pairs).astype(F32)  2.48 us
  transfers between devices with their start and end apart: 1, of which 1 were waited for; matrix products, arithmetic and copies ran while one was open for 1% of the time, Pallas kernels for 0%

profile of v2, /device:TPU:25, one launch (start us, length us, event | category | flops | bytes accessed | tf_op | source)
XLA Modules:
  0.0 59.2 jit_solution(4731606456869586413)
XLA Ops:
  0.6 0.0 copy-start.11
  0.6 0.0 copy-start.10
  0.7 1.0 %convert_element_type.10 = bf16[2,49,384]{2,0,1:T(2,128)(2,1)S(1)} convert(f32[2,49,384]{2,0,1:T(2,128)} %param.8) | non-fusion elementwise | flops 37632 | bytes 225792 | tf_op jit(solution)/shard_map/convert_element_type | solution.py:307
  1.7 0.1 reshape.45
  1.8 0.1 copy.23
  1.9 0.1 broadcast_in_dim.12
  2.0 0.3 broadcast_in_dim.13
  2.4 0.0 copy-done.11
  2.4 0.1 copy.22
  2.5 0.0 copy-done.10
  2.5 0.2 copy.31
  2.7 0.0 copy-start.1
  2.7 0.1 fusion.32
  2.8 0.2 broadcast_in_dim.14.coef_ref
  2.9 0.8 %copy-done.1 = bf16[2,384,384]{2,1,0:T(8,128)(2,1)S(1)} copy-done((bf16[2,384,384]{2,1,0:T(8,128)(2,1)S(1)}, bf16[2,384,384]{2,1,0:T(8,128)(2,1)}, u32[]{:S(2)}) %copy-start.1) | copy-done | bytes 589848
  3.8 0.0 copy-start
  3.8 2.5 %copy-done = bf16[2,3,3,384,384]{4,3,2,1,0:T(8,128)(2,1)S(1)} copy-done((bf16[2,3,3,384,384]{4,3,2,1,0:T(8,128)(2,1)S(1)}, bf16[2,3,3,384,384]{4,3,2,1,0:T(8,128)(2,1)}, u32[]{:S(2)}) %copy-start) | copy-done | bytes 5308440
  6.3 12.3 %tick.4 = (bf16[256,384]{1,0:T(8,128)(2,1)}, bf16[256,384]{1,0:T(8,128)(2,1)S(1)}, bf16[256,384]{1,0:T(8,128)(2,1)S(1)}, bf16[256,384]{1,0:T(8,128)(2,1)S(1)}, b...) custom-call(s32[1]{0:T(128)} %bitcast.lead_ref, ...), custom_call_target="tpu_custom_call" | custom-call | flops 10000000000 | bytes 786432 | tf_op jit(solution)/shard_map/tick/pallas_call | solution.py:278
  18.6 10.0 %tick.5 = (bf16[256,384]{1,0:T(8,128)(2,1)}, bf16[256,384]{1,0:T(8,128)(2,1)S(1)}, bf16[256,384]{1,0:T(8,128)(2,1)S(1)}, bf16[256,384]{1,0:T(8,128)(2,1)S(1)}, b...) custom-call(s32[1]{0:T(128)} %bitcast.lead_ref, ...), custom_call_target="tpu_custom_call" | custom-call | flops 10000000000 | bytes 786432 | tf_op jit(solution)/shard_map/tick/pallas_call | solution.py:278
  28.5 10.4 %tick.6 = (bf16[256,384]{1,0:T(8,128)(2,1)}, bf16[256,384]{1,0:T(8,128)(2,1)S(1)}, bf16[256,384]{1,0:T(8,128)(2,1)S(1)}, bf16[256,384]{1,0:T(8,128)(2,1)S(1)}, b...) custom-call(s32[1]{0:T(128)} %bitcast.lead_ref, ...), custom_call_target="tpu_custom_call" | custom-call | flops 10000000000 | bytes 786432 | tf_op jit(solution)/shard_map/tick/pallas_call | solution.py:278
  39.0 0.0 copy-start.6
  39.0 0.0 copy-start.7
  39.0 8.1 %tick.7 = (bf16[256,384]{1,0:T(8,128)(2,1)S(1)}, bf16[256,384]{1,0:T(8,128)(2,1)S(1)}, bf16[256,384]{1,0:T(8,128)(2,1)S(1)}, bf16[256,384]{1,0:T(8,128)(2,1)S(1)...) custom-call(s32[1]{0:T(128)} %bitcast.lead_ref, bf16[256,384]{1,0:T(8,128)(2,1)S(1)} %bitcast.39, ...), custom_call_target="tpu_custom_call" | custom-call | flops 10000000000 | bytes 786432 | tf_op jit(solution)/shard_map/tick/pallas_call | solution.py:278
  47.1 0.0 copy-done.6
  47.1 0.0 copy-done.7
  47.1 0.0 copy-start.2
  47.1 0.7 %copy-done.2 = bf16[256,384]{1,0:T(8,128)(2,1)} copy-done((bf16[256,384]{1,0:T(8,128)(2,1)}, bf16[256,384]{1,0:T(8,128)(2,1)S(1)}, u32[]{:S(2)}) %copy-start.2) | copy-done | bytes 196632
  47.8 0.0 copy-start.4
  47.8 0.7 %copy-done.4 = bf16[256,384]{1,0:T(8,128)(2,1)} copy-done((bf16[256,384]{1,0:T(8,128)(2,1)}, bf16[256,384]{1,0:T(8,128)(2,1)S(1)}, u32[]{:S(2)}) %copy-start.4) | copy-done | bytes 196632
  48.4 0.0 copy-start.8
  48.4 0.7 %copy-done.8 = bf16[256,384]{1,0:T(8,128)(2,1)} copy-done((bf16[256,384]{1,0:T(8,128)(2,1)}, bf16[256,384]{1,0:T(8,128)(2,1)S(1)}, u32[]{:S(2)}) %copy-start.8) | copy-done | bytes 196632
  49.1 0.0 copy-start.9
  49.1 0.7 %copy-done.9 = bf16[256,384]{1,0:T(8,128)(2,1)} copy-done((bf16[256,384]{1,0:T(8,128)(2,1)}, bf16[256,384]{1,0:T(8,128)(2,1)S(1)}, u32[]{:S(2)}) %copy-start.9) | copy-done | bytes 196632
  49.8 0.3 reduce_sum.9
  50.1 0.1 copy.26
  50.2 0.0 copy-start.3
  50.2 0.0 copy-start.5
  50.3 1.9 %fusion = f32[384,384]{0,1:T(8,128)S(1)} fusion(bf16[256,384]{1,0:T(8,128)(2,1)} %copy-done.9, bf16[256,384]{1,0:T(8,128)(2,1)} %copy-done.7, bf16[256,384]{1,0:T(8,128)(2,1)S(1)} %get-tuple-element.35, bf16[256,384]{1,0:T(8,128)(2,1)S(1)} %get-tuple-element.34, bf16[256,384]{1,0:T(8,128)(2,1)} %copy-done.8, bf16[256,384]{1,0:T(8,128)(2,1)} %copy-done.6, ...), kind=kOutput, calls=%fused_computation.3 | convolution fusion | flops 308281344 | bytes 2162688 | tf_op jit(solution)/shard_map/dot_general | solution.py:325
  52.1 0.0 copy-done.3
  52.1 0.0 copy-done.5
  52.2 0.6 %fusion.15 = f32[384,384]{0,1:T(8,128)S(1)} fusion(bf16[256,384]{1,0:T(8,128)(2,1)S(1)} %copy-done.5, bf16[256,384]{1,0:T(8,128)(2,1)S(1)} %get-tuple-element.44, bf16[256,384]{1,0:T(8,128)(2,1)S(1)} %get-tuple-element.43, bf16[256,384]{1,0:T(8,128)(2,1)S(1)} %get-tuple-element.42, bf16[256,384]{1,0:T(8,128)(2,1)S(1)} %copy-done.3, ...), kind=kOutput, calls=%fused_computation.18 | convolution fusion | flops 308281344 | bytes 2162688 | tf_op jit(solution)/shard_map/dot_general | solution.py:325
  52.8 0.1 pad_maximum_fusion
  52.9 0.2 dynamic-slice_convert_fusion
  53.1 2.5 %collective-permute-start = (bf16[192,866]{0,1:T(8,128)(2,1)S(1)}, bf16[192,866]{0,1:T(8,128)(2,1)S(1)}, u32[]{:S(2)}, u32[]{:S(2)}) collective-permute-start(bf16[192,866]{0,1:T(8,128)(2,1)S(1)} %dynamic-slice_convert_fusion), channel_id=1, source_target_pairs={{0,1},{1,0},{2,3},{3,2},{4,5},{5,4},{6,7},{7,6},{8,9},{9,8},{10,11... | collective-permute-start | bytes 997640 | tf_op jit(solution)/shard_map/ppermute | solution.py:337
  55.6 0.7 %copy.25 = bf16[8,2,16,384]{3,2,1,0:T(8,128)(2,1)} copy(bf16[8,2,16,384]{3,0,1,2:T(8,128)(2,1)S(1)} %bitcast.42) | data formatting | bytes 393216 | tf_op jit(solution)/shard_map/transpose | solution.py:340
  56.3 0.7 %collective-permute-done = bf16[192,866]{0,1:T(8,128)(2,1)S(1)} collective-permute-done((bf16[192,866]{0,1:T(8,128)(2,1)S(1)}, bf16[192,866]{0,1:T(8,128)(2,1)S(1)}, u32[]{:S(2)}, u32[]{:S(2)}) %collective-permute-start) | collective-permute-done | bytes 332576 | tf_op jit(solution)/shard_map/ppermute | solution.py:337
  57.0 0.3 convert_add_fusion
  57.3 0.1 slice_bitcast_fusion.1
  57.4 0.1 maximum_bitcast_fusion
  57.4 1.1 %copy.27 = f32[2,384,192]{1,2,0:T(8,128)} copy(f32[2,384,192]{2,1,0:T(8,128)S(1)} %maximum_bitcast_fusion) | data formatting | bytes 1179648
  58.5 0.7 %copy.28 = f32[2,49,192]{2,0,1:T(2,128)} copy(f32[2,49,192]{2,1,0:T(8,128)S(1)} %reshape.49) | data formatting | bytes 150528
  (5 shorter events, 0.1 us)
Async XLA Ops:
  0.6 1.8 %copy-start.11 = (bf16[1,1,8,32,384]{4,3,2,1,0:T(8,128)(2,1)S(1)}, bf16[1,1,8,32,384]{4,3,2,1,0:T(8,128)(2,1)}, u32[]{:S(2)}) copy-start(bf16[1,1,8,32,384]{4,3,2,1,0:T(8,128)(2,1)} %param.5) | copy-start | bytes 589828
  0.6 1.8 %copy-start.10 = (bf16[3,1,8,32,384]{4,3,2,1,0:T(8,128)(2,1)S(1)}, bf16[3,1,8,32,384]{4,3,2,1,0:T(8,128)(2,1)}, u32[]{:S(2)}) copy-start(bf16[3,1,8,32,384]{4,3,2,1,0:T(8,128)(2,1)} %param.6) | copy-start | bytes 1769476
  2.7 1.1 %copy-start.1 = (bf16[2,384,384]{2,1,0:T(8,128)(2,1)S(1)}, bf16[2,384,384]{2,1,0:T(8,128)(2,1)}, u32[]{:S(2)}) copy-start(bf16[2,384,384]{2,1,0:T(8,128)(2,1)} %point_ref.7) | copy-start | bytes 1769476
  3.8 2.5 %copy-start = (bf16[2,3,3,384,384]{4,3,2,1,0:T(8,128)(2,1)S(1)}, bf16[2,3,3,384,384]{4,3,2,1,0:T(8,128)(2,1)}, u32[]{:S(2)}) copy-start(bf16[2,3,3,384,384]{4,3,2,1,0:T(8,128)(2,1)} %param.7) | copy-start | bytes 15925252
  39.0 8.1 %copy-start.6 = (bf16[256,384]{1,0:T(8,128)(2,1)}, bf16[256,384]{1,0:T(8,128)(2,1)S(1)}, u32[]{:S(2)}) copy-start(bf16[256,384]{1,0:T(8,128)(2,1)S(1)} %get-tuple-element.40) | copy-start | bytes 589828
  39.0 8.1 %copy-start.7 = (bf16[256,384]{1,0:T(8,128)(2,1)}, bf16[256,384]{1,0:T(8,128)(2,1)S(1)}, u32[]{:S(2)}) copy-start(bf16[256,384]{1,0:T(8,128)(2,1)S(1)} %get-tuple-element.36) | copy-start | bytes 589828
  47.1 0.7 %copy-start.2 = (bf16[256,384]{1,0:T(8,128)(2,1)}, bf16[256,384]{1,0:T(8,128)(2,1)S(1)}, u32[]{:S(2)}) copy-start(bf16[256,384]{1,0:T(8,128)(2,1)S(1)} %get-tuple-element.49) | copy-start | bytes 589828
  47.8 0.7 %copy-start.4 = (bf16[256,384]{1,0:T(8,128)(2,1)}, bf16[256,384]{1,0:T(8,128)(2,1)S(1)}, u32[]{:S(2)}) copy-start(bf16[256,384]{1,0:T(8,128)(2,1)S(1)} %get-tuple-element.45) | copy-start | bytes 589828
  48.4 0.7 %copy-start.8 = (bf16[256,384]{1,0:T(8,128)(2,1)}, bf16[256,384]{1,0:T(8,128)(2,1)S(1)}, u32[]{:S(2)}) copy-start(bf16[256,384]{1,0:T(8,128)(2,1)S(1)} %get-tuple-element.41) | copy-start | bytes 589828
  49.1 0.7 %copy-start.9 = (bf16[256,384]{1,0:T(8,128)(2,1)}, bf16[256,384]{1,0:T(8,128)(2,1)S(1)}, u32[]{:S(2)}) copy-start(bf16[256,384]{1,0:T(8,128)(2,1)S(1)} %get-tuple-element.37) | copy-start | bytes 589828
  50.2 1.9 %copy-start.3 = (bf16[256,384]{1,0:T(8,128)(2,1)S(1)}, bf16[256,384]{1,0:T(8,128)(2,1)}, u32[]{:S(2)}) copy-start(bf16[256,384]{1,0:T(8,128)(2,1)} %copy-done.2) | copy-start | bytes 589828
  50.2 1.9 %copy-start.5 = (bf16[256,384]{1,0:T(8,128)(2,1)S(1)}, bf16[256,384]{1,0:T(8,128)(2,1)}, u32[]{:S(2)}) copy-start(bf16[256,384]{1,0:T(8,128)(2,1)} %copy-done.4) | copy-start | bytes 589828
  53.1 3.9 %collective-permute-start = (bf16[192,866]{0,1:T(8,128)(2,1)S(1)}, bf16[192,866]{0,1:T(8,128)(2,1)S(1)}, u32[]{:S(2)}, u32[]{:S(2)}) collective-permute-start(bf16[192,866]{0,1:T(8,128)(2,1)S(1)} %dynamic-slice_convert_fusion), channel_id=1, source_target_pairs={{0,1},{1,0},{2,3},{3,2},{4,5},{5,4},{6,7},{7,6},{8,9},{9,8},{10,11... | collective-permute-start | bytes 997640 | tf_op jit(solution)/shard_map/ppermute | solution.py:337

commit v3 on v2

v3 whole, which is shorter than its diff:
```python
import functools

import jax
import jax.numpy as jnp
from jax import lax
from jax.experimental import pallas as pl
from jax.experimental.pallas import tpu as pltpu
from jax.sharding import PartitionSpec as P

LANES = 128
F32 = jnp.float32
BF16 = jnp.bfloat16
MESH = pl.DeviceIdType.MESH
NT = (((1,), (1,)), ((), ()))
TN = (((0,), (0,)), ((), ()))
SIDE = 7


def lanes(block):
    return slice(block * LANES, (block + 1) * LANES)


def columns(block):
    return pl.ds(pl.multiple_of(block * LANES, LANES), LANES)


def put_padded(vals, pad_ref, height):
    units = vals.shape[0] // (2 * height)
    for block in range(vals.shape[1] // LANES):
        for unit in range(units):
            for half in range(2):
                at = (2 * unit + half) * height
                to = (2 * (unit + half * units) + 1) * height
                pad_ref[block, to : to + height] = vals[at : at + height, lanes(block)]


def get_padded(pad_ref, block, height, units):
    rows = []
    for unit in range(units):
        for half in range(2):
            at = (2 * (unit + half * units) + 1) * height
            rows.append(pad_ref[block, at : at + height])
    return jnp.concatenate(rows, axis=0)


def spread(pad_ref, put, height, units, reach):
    def one_row(row, carry):
        for block in range(pad_ref.shape[0]):

            def load(w):
                return pad_ref[block, pl.ds((2 * w + 1) * height + row - reach, height)]

            zero = jnp.zeros((height, LANES), F32)
            cols = [load(w) for w in range(2 * units)]
            low = [zero] * reach + cols[: units + reach]
            high = cols[units - reach :] + [zero] * reach
            for unit in range(units + 2 * reach):
                put(block, row, unit, low[unit], high[unit])
        return carry

    lax.fori_loop(0, 2 * reach + 1, one_row, 0)


def strips(out_ref):
    def put(block, row, unit, low, high):
        out_ref[block, row, unit] = jnp.concatenate([low, high], axis=1).astype(BF16)

    return put


def windows(out_ref, height):
    def put(block, row, unit, low, high):
        at = slice(unit * 2 * height, (unit + 1) * 2 * height)
        out_ref[row, at, lanes(block)] = jnp.concatenate([low, high], axis=0).astype(BF16)

    return put


def beside(vals, height):
    split = vals.reshape(-1, 2 * height, LANES)
    return jnp.concatenate([split[:, :height], split[:, height:]], axis=2)


def below(vals):
    return jnp.concatenate([vals[:, :, :LANES], vals[:, :, LANES:]], axis=1).reshape(-1, LANES)


def tap_sum(src_ref, block, coef_ref, which, start, count, flip):
    total = None
    for rows in ((0, 1, 2, 3), (4, 5, 6)):
        part = None
        for row in rows:
            strip = src_ref[block, row, pl.ds(start, count + 6)]
            acc = None
            for col in range(SIDE):
                tap = row * SIDE + col
                tap = 48 - tap if flip else tap
                term = strip[col : col + count] * coef_ref[which, block, tap][None]
                acc = term if acc is None else acc + term
            part = acc if part is None else part + acc
        wide = part.astype(F32)
        total = wide if total is None else total + wide
    return total


def gelu_pair(act):
    root = 0.7978845608028654
    cubic = root * 0.044715
    square = act * act
    tanh = jnp.tanh(act * (root + cubic * square))
    half = 0.5 + 0.5 * tanh
    slope = half + (half - half * half) * (act * (2.0 * root + 6.0 * cubic * square))
    return act * half, slope


def step_kernel(
    height, step, ticks, sections, parties,
    pipe_hbm, fresh_hbm, weight_hbm, taps_ref, point_hbm,
    final_ref, pg_ref, pg_in_ref, dk_ref, dk_in_ref,
    raw, weight, point, raw_sem, weight_sem, point_sem,
    teach, land, send_sem, recv_sem,
    pg_out, pg_land, dk_out, dk_land, swap_send, swap_recv,
    coef, pad, hpad, src0, src1, src2, win, slope0, slope1, dact0, cur, u_one, resid, gels, grads, sums,
):
    rows, chans = cur.shape
    blocks = chans // LANES
    pair = 2 * height
    units = rows // pair
    chunks = units // step
    share = chans // parties
    srcs, slopes = (src0, src1), (slope0, slope1)
    spot, me = lax.axis_index("section"), lax.axis_index("dp")
    barrier = pltpu.get_barrier_semaphore()

    @pl.when(spot > 0)
    def _():
        pl.semaphore_signal(barrier, inc=1, device_id={"section": spot - 1}, device_id_type=MESH)

    for hop in range(1, parties):
        peer = lax.rem(me + hop, parties)
        pl.semaphore_signal(barrier, inc=1, device_id={"dp": peer}, device_id_type=MESH)

    fetch_pipe = pltpu.make_async_copy(pipe_hbm, raw.at[0], raw_sem.at[0])
    fetch_fresh = pltpu.make_async_copy(fresh_hbm, raw.at[pl.ds(1, ticks - 1)], raw_sem.at[1])
    fetch_weight = [pltpu.make_async_copy(weight_hbm.at[i], weight.at[i], weight_sem.at[i]) for i in range(2)]
    fetch_point = pltpu.make_async_copy(point_hbm, point, point_sem)
    for fetch in (fetch_pipe, fetch_weight[0], fetch_weight[1], fetch_point, fetch_fresh):
        fetch.start()

    def span(index):
        return pl.ds(pl.multiple_of(index * step * pair, step * pair), step * pair)

    zero = jnp.zeros((height, LANES), F32)
    for block in range(blocks):
        for at in range(0, pad.shape[1], pair):
            pad[block, at : at + height] = zero
            hpad[block, at : at + height] = zero
    for which in range(2):
        for block in range(blocks):
            for tap in range(SIDE * SIDE):
                line = jnp.broadcast_to(taps_ref[tap, which : which + 1, lanes(block)], (height, LANES))
                coef[which, block, tap] = jnp.concatenate([line, line], axis=1).astype(BF16)
    sums[...] = jnp.zeros_like(sums)

    def take_raw(tick):
        for row in range(height):
            line = raw[tick, row].astype(F32)
            for block in range(blocks):
                pad[block, pl.ds(height + row, 2 * units, stride=pair)] = line[:, lanes(block)]

    def keep_input():
        for block in range(blocks):
            cur[:, lanes(block)] = get_padded(pad, block, height, units)
        spread(pad, windows(win, height), height, units, 1)

    def conv(which):
        parts = [win[down, right * pair : right * pair + rows] for down in range(3) for right in range(3)]
        return jnp.dot(jnp.concatenate(parts, axis=1), weight[which], preferred_element_type=F32)

    def keep_hidden(hidden):
        put_padded(jnp.maximum(hidden, 0.0), hpad, height)
        spread(hpad, windows(win, height), height, units, 1)

    def keep_teach(second, tick):
        teach[tick] = (0.8 * (cur[...] + second)).astype(BF16)

    def relay(tick):
        return pltpu.make_async_remote_copy(
            src_ref=teach.at[tick],
            dst_ref=land.at[tick],
            send_sem=send_sem.at[tick],
            recv_sem=recv_sem.at[tick],
            device_id={"section": lax.rem(spot + 1, sections)},
            device_id_type=MESH,
        )

    def send(tick):
        @pl.when(spot < sections - 1)
        def _():
            relay(tick).start()

    def back_point(which, tick):
        dgel = lax.dot_general(grads[which, tick], point[which], NT, preferred_element_type=F32)
        return dgel * slopes[which][...]

    def forward(which, tick):
        def chunk(at, carry):
            block, index = at // chunks, lax.rem(at, chunks)
            act = tap_sum(srcs[which], block, coef, which, index * step, step, False)
            gel, slope = gelu_pair(below(act))
            slopes[which][span(index), columns(block)] = slope
            gels[which, tick, span(index), columns(block)] = gel.astype(BF16)
            return carry

        lax.fori_loop(0, blocks * chunks, chunk, 0)
        return jnp.dot(gels[which, tick], point[which], preferred_element_type=F32)

    def student(tick):
        spread(pad, strips(src0), height, units, 3)
        middle = forward(0, tick) + cur[...]
        u_one[...] = middle
        put_padded(middle, pad, height)
        spread(pad, strips(src1), height, units, 3)
        diff = forward(1, tick) + u_one[...] - teach[tick].astype(F32)
        left = diff * (4.0 / rows)
        resid[...] = left
        grads[1, tick] = left.astype(BF16)
        put_padded(back_point(1, tick), pad, height)
        spread(pad, strips(src2), height, units, 3)

        def chunk_back(at, carry):
            block, index = at // chunks, lax.rem(at, chunks)
            back = tap_sum(src2, block, coef, 1, index * step, step, True)
            back = below(back) + resid[span(index), columns(block)]
            grads[0, tick, span(index), columns(block)] = back.astype(BF16)
            return carry

        lax.fori_loop(0, blocks * chunks, chunk_back, 0)
        dact = back_point(0, tick)
        for block in range(blocks):
            dact0[block] = beside(dact[:, lanes(block)], height).astype(BF16)

    def taps_grad(which):
        for block in range(blocks):
            part = src2[block, 3, 3 : 3 + units] if which else dact0[block]
            for row in range(SIDE):
                strip = srcs[which][block, row]
                for col in range(SIDE):
                    prod = strip[col : col + units] * part
                    size = units
                    while size > 1:
                        size //= 2
                        prod = prod[:size] + prod[size:]
                    wide = prod[0].astype(F32)
                    sums[which, block, row, col] += wide[:, :LANES] + wide[:, LANES:]

    fetch_pipe.wait()
    take_raw(0)
    keep_input()
    fetch_weight[0].wait()
    keep_hidden(conv(0))
    fetch_weight[1].wait()
    keep_teach(conv(1), 0)
    pl.semaphore_wait(barrier, parties - 1 + (spot < sections - 1).astype(jnp.int32))
    send(0)
    fetch_point.wait()
    fetch_fresh.wait()

    def tick_body(tick, carry):
        student(tick)

        @pl.when(spot > 0)
        def _():
            relay(tick).wait_recv()
            put_padded(land[tick].astype(F32), pad, height)

        @pl.when(spot == 0)
        def _():
            take_raw(tick + 1)

        keep_input()
        hidden = conv(0)
        taps_grad(1)
        keep_hidden(hidden)
        second = conv(1)
        taps_grad(0)
        keep_teach(second, tick + 1)

        @pl.when(tick + 1 < ticks - 1)
        def _():
            send(tick + 1)

        return carry

    lax.fori_loop(0, ticks - 1, tick_body, 0)
    last = ticks - 1
    for block in range(blocks):
        hpad_rows = teach[last, :, lanes(block)].astype(F32)
        for unit in range(units):
            for half in range(2):
                at = (2 * unit + half) * height
                to = (2 * (unit + half * units) + 1) * height
                hpad[block, to : to + height] = hpad_rows[at : at + height]
    for row in range(height):
        parts = [hpad[block, pl.ds(height + row, 2 * units, stride=pair)] for block in range(blocks)]
        final_ref[row] = jnp.concatenate(parts, axis=1).astype(BF16)
    student(last)

    def swap(hop, which):
        src, dst = (dk_out, dk_land.at[hop - 1]) if which == 2 else (None, None)
        peer = lax.rem(me + hop, parties)
        if src is None:
            src = pg_out.at[which, pl.ds(pl.multiple_of(peer * share, 16), share)]
            dst = pg_land.at[hop - 1, which]
        return pltpu.make_async_remote_copy(
            src_ref=src,
            dst_ref=dst,
            send_sem=swap_send.at[hop - 1, which],
            recv_sem=swap_recv.at[hop - 1, which],
            device_id={"dp": peer},
            device_id_type=MESH,
        )

    def point_grad(which):
        up = grads[which].reshape(ticks * rows, chans)
        total = lax.dot_general(up, gels[which].reshape(ticks * rows, chans), TN, preferred_element_type=F32)
        pg_ref[which] = total
        pg_out[which] = total.astype(BF16)

    point_grad(1)
    taps_grad(1)
    for hop in range(1, parties):
        swap(hop, 1).start()
    point_grad(0)
    taps_grad(0)
    for hop in range(1, parties):
        swap(hop, 0).start()
    for which in range(2):
        for block in range(blocks):
            for row in range(SIDE):
                line = jnp.sum(sums[which, block, row], axis=1)
                at = slice(row * SIDE, (row + 1) * SIDE)
                dk_ref[which, at, lanes(block)] = line
    dk_out[...] = dk_ref[...].astype(BF16)
    for hop in range(1, parties):
        swap(hop, 2).start()
    for which in (1, 0, 2):
        for hop in range(1, parties):
            swap(hop, which).wait_recv()
    pg_in_ref[...] = pg_land[...]
    dk_in_ref[...] = dk_land[...]
    for which in (1, 0, 2):
        for hop in range(1, parties):
            swap(hop, which).wait_send()

    @pl.when(spot < sections - 1)
    def _():
        for tick in range(ticks - 1):
            relay(tick).wait_send()


def finish_kernel(parties, final_in, pg_ref, pg_in_ref, dk_ref, dk_in_ref, final_ref, point_ref, depth_ref):
    me = lax.axis_index("dp")
    share = point_ref.shape[1]
    final_ref[...] = final_in[...]
    for which in range(2):
        total = pg_ref[which, pl.ds(pl.multiple_of(me * share, 16), share)]
        for hop in range(parties - 1):
            total = total + pg_in_ref[hop, which].astype(F32)
        point_ref[which] = total
        depth = dk_ref[which]
        for hop in range(parties - 1):
            depth = depth + dk_in_ref[hop, which].astype(F32)
        for party in range(parties):

            @pl.when(me == party)
            def _():
                depth_ref[which] = depth[:, party * share : (party + 1) * share]


def body(pipe_maps, fresh_maps, teacher_weight, student_depth, student_point):
    _, _, height, width, chans = pipe_maps.shape
    rows = height * width
    blocks = chans // LANES
    pair = 2 * height
    units = rows // pair
    ticks = fresh_maps.shape[0] + 1
    sections, parties = lax.axis_size("section"), lax.axis_size("dp")
    share = chans // parties
    peers = max(parties - 1, 1)
    hbm = pl.BlockSpec(memory_space=pl.ANY)
    vmem = pl.BlockSpec(memory_space=pltpu.VMEM)
    dma = pltpu.SemaphoreType.DMA
    pad_shape = pltpu.VMEM((blocks, (2 * width + 1) * height, LANES), F32)
    src_shape = pltpu.VMEM((blocks, SIDE, units + 6, height, 2 * LANES), BF16)
    map_shape = pltpu.VMEM((rows, chans), F32)
    taps = SIDE * SIDE
    results = (
        jax.ShapeDtypeStruct((height, width, chans), BF16),
        jax.ShapeDtypeStruct((2, chans, chans), F32),
        jax.ShapeDtypeStruct((peers, 2, share, chans), BF16),
        jax.ShapeDtypeStruct((2, taps, chans), F32),
        jax.ShapeDtypeStruct((peers, 2, taps, chans), BF16),
    )
    outs = pl.pallas_call(
        functools.partial(step_kernel, height, units // 2, ticks, sections, parties),
        out_shape=results,
        in_specs=[hbm, hbm, hbm, vmem, hbm],
        out_specs=(vmem,) * len(results),
        scratch_shapes=[
            pltpu.VMEM((ticks, height, width, chans), BF16),
            pltpu.VMEM((2, 9 * chans, chans), BF16),
            pltpu.VMEM((2, chans, chans), BF16),
            dma((2,)),
            dma((2,)),
            dma,
            pltpu.VMEM((ticks, rows, chans), BF16),
            pltpu.VMEM((ticks - 1, rows, chans), BF16),
            dma((ticks - 1,)),
            dma((ticks - 1,)),
            pltpu.VMEM((2, chans, chans), BF16),
            pltpu.VMEM((peers, 2, share, chans), BF16),
            pltpu.VMEM((2, taps, chans), BF16),
            pltpu.VMEM((peers, 2, taps, chans), BF16),
            dma((peers, 3)),
            dma((peers, 3)),
            pltpu.VMEM((2, blocks, taps, height, 2 * LANES), BF16),
            pad_shape,
            pad_shape,
            src_shape,
            src_shape,
            src_shape,
            pltpu.VMEM((3, (units + 2) * pair, chans), BF16),
            map_shape,
            map_shape,
            pltpu.VMEM((blocks, units, height, 2 * LANES), BF16),
            map_shape,
            map_shape,
            map_shape,
            pltpu.VMEM((2, ticks, rows, chans), BF16),
            pltpu.VMEM((2, ticks, rows, chans), BF16),
            pltpu.VMEM((2, blocks, SIDE, SIDE, height, LANES), F32),
        ],
        compiler_params=pltpu.CompilerParams(
            vmem_limit_bytes=44 << 20, collective_id=0, has_side_effects=True
        ),
        name="step",
    )(
        pipe_maps[0, 0],
        fresh_maps[:, 0],
        teacher_weight.reshape(2, 9 * chans, chans),
        student_depth.swapaxes(0, 1),
        student_point,
    )
    final, point_grad, depth_grad = pl.pallas_call(
        functools.partial(finish_kernel, parties),
        out_shape=(
            results[0],
            jax.ShapeDtypeStruct((2, share, chans), F32),
            jax.ShapeDtypeStruct((2, taps, share), F32),
        ),
        in_specs=[vmem] * len(outs),
        out_specs=(vmem,) * 3,
        name="finish",
    )(*outs)
    return final[None, None], point_grad.swapaxes(1, 2), depth_grad


def solution(mesh):
    placed = (
        P("section", "dp", None, None, None),
        P(None, "dp", None, None, None),
        P("section", None, None, None, None),
        P("section", None, None),
        P("section", None, None),
    )
    return jax.shard_map(
        body,
        mesh=mesh,
        in_specs=placed,
        out_specs=(
            P("section", "dp", None, None, None),
            P("section", None, "dp"),
            P("section", None, "dp"),
        ),
        check_vma=False,
    )
```

time: 59.5 us -> 56.7 us (0.953)
  Pallas kernels: 40.7 us -> 43.9 us
  matrix products: 2.5 us -> 0 us
  starting transfers between devices: 2.48 us -> 0 us
  other arithmetic: 1.79 us -> 0 us
  local copies, waits for them, and re-layouts: 10.1 us -> 11.8 us
  waiting for transfers between devices: 0.71 us -> 0 us
    unnamed x28 -> x21, local copies, waits for them, and re-layouts: 7.87 us -> 11.8 us
    pallas_call x4 -> x2, Pallas kernels: 40.7 us -> 43.9 us  [the longest x1 41.3 us: body(): pl.pallas_call(functools.partial(step_kernel, height, units // 2, ticks,...]
    dot_general x2 -> x0, matrix products: 2.5 us -> none  [body(): lax.dot_general(grad_all[b], gel_all[b], (((0,), (0,)), ((), ())), prefer...]
    ppermute x1 -> x0, starting transfers between devices: 2.48 us -> none  [body(): total = total + lax.ppermute(out.astype(BF16), 'dp', pairs).astype(F32)]
    convert_element_type x1 -> x0, other arithmetic: 1.04 us -> none  [body(): student_depth.astype(BF16).reshape(2, 49, blocks, 1, 1, LANES)]
    transpose x3 -> x0, local copies, waits for them, and re-layouts: 0.78 us -> none  [the longest x1 0.71 us: body(): final = jnp.swapaxes(teach.reshape(width // 2, 2, height, chans), 0, 2)]
    ppermute x1 -> x0, waiting for transfers between devices: 0.71 us -> none  [body(): total = total + lax.ppermute(out.astype(BF16), 'dp', pairs).astype(F32)]
    broadcast_in_dim x5 -> x0, local copies, waits for them, and re-layouts: 0.69 us -> none  [body(): jnp.broadcast_to(coef, (2, blocks, 49, height, 2, LANES))]
  transfers between devices with their start and end apart: 1 -> 0, of which waited for: 1 -> 0; matrix products, arithmetic and copies ran while one was open for 1% -> 0% of each run, Pallas kernels for 0% -> 0%
where the time goes in v3:
time: 56.7 us; the launch traced here: 56.3 us
  Pallas kernels  43.9 us (77%)
  local copies, waits for them, and re-layouts  11.8 us (21%)
  between operations  0.67 us (1%)
    pallas_call x1, Pallas kernels, body(): pl.pallas_call(functools.partial(step_kernel, height, units // 2, ticks,...  41.3 us
    unnamed x21, local copies, waits for them, and re-layouts  11.8 us
    pallas_call x1, Pallas kernels, body(): pl.pallas_call(functools.partial(finish_kernel, parties), out_shape=(resu...  2.59 us

profile of v3, /device:TPU:25, one launch (start us, length us, event | category | flops | bytes accessed | tf_op | source)
XLA Modules:
  0.0 56.3 jit_solution(6412386945788491888)
XLA Ops:
  0.6 0.0 copy-start
  0.6 2.5 %copy-done = bf16[2,3,3,384,384]{4,3,2,1,0:T(8,128)(2,1)S(1)} copy-done((bf16[2,3,3,384,384]{4,3,2,1,0:T(8,128)(2,1)S(1)}, bf16[2,3,3,384,384]{4,3,2,1,0:T(8,128)(2,1)}, u32[]{:S(2)}) %copy-start) | copy-done | bytes 5308440
  3.1 0.0 copy-start.2
  3.1 1.1 %copy-done.2 = bf16[3,1,8,32,384]{4,3,2,1,0:T(8,128)(2,1)S(1)} copy-done((bf16[3,1,8,32,384]{4,3,2,1,0:T(8,128)(2,1)S(1)}, bf16[3,1,8,32,384]{4,3,2,1,0:T(8,128)(2,1)}, u32[]{:S(2)}) %copy-start.2) | copy-done | bytes 589848
  4.2 0.0 copy-start.3
  4.2 1.1 %copy-done.3 = bf16[2,384,384]{2,1,0:T(8,128)(2,1)S(1)} copy-done((bf16[2,384,384]{2,1,0:T(8,128)(2,1)S(1)}, bf16[2,384,384]{2,1,0:T(8,128)(2,1)}, u32[]{:S(2)}) %copy-start.3) | copy-done | bytes 589848
  5.3 0.0 copy-start.5
  5.3 0.9 %copy-done.5 = bf16[1,1,8,32,384]{4,3,2,1,0:T(8,128)(2,1)S(1)} copy-done((bf16[1,1,8,32,384]{4,3,2,1,0:T(8,128)(2,1)S(1)}, bf16[1,1,8,32,384]{4,3,2,1,0:T(8,128)(2,1)}, u32[]{:S(2)}) %copy-start.5) | copy-done | bytes 196632
  6.2 0.0 copy-start.8
  6.2 0.9 %copy-done.8 = f32[2,49,384]{2,0,1:T(2,128)S(1)} copy-done((f32[2,49,384]{2,0,1:T(2,128)S(1)}, f32[2,49,384]{2,0,1:T(2,128)}, u32[]{:S(2)}) %copy-start.8) | copy-done | bytes 150552
  7.1 41.3 %step.1 = (bf16[8,32,384]{2,1,0:T(8,128)(2,1)S(1)}, f32[2,384,384]{2,1,0:T(8,128)S(1)}, bf16[1,2,192,384]{3,2,1,0:T(8,128)(2,1)S(1)}, f32[2,49,384]{2,1,0:T(8,128)S(1)}, bf16[1,2,49,384]{3,2,1,0:T(8,128)(2,1)S(1)}) custom-call(bf16[8,32,384]{2,1,0:T(8,128)(2,1)S(1)} %bitcast.8, bf16[3,8,32,384]{3,2,1,0:T(8,128)(2,1)S(1)} %bitcast.7, ...), custom_call_target="tpu_custom_call" | custom-call | tf_op jit(solution)/shard_map/step/pallas_call | solution.py:405
  48.4 0.0 copy-start.1
  48.4 1.0 %copy-done.1 = f32[2,384,384]{2,1,0:T(8,128)} copy-done((f32[2,384,384]{2,1,0:T(8,128)}, f32[2,384,384]{2,1,0:T(8,128)S(1)}, u32[]{:S(2)}) %copy-start.1) | copy-done | bytes 1179672
  49.4 0.0 copy-start.4
  49.4 0.7 %copy-done.4 = bf16[1,2,192,384]{3,2,1,0:T(8,128)(2,1)} copy-done((bf16[1,2,192,384]{3,2,1,0:T(8,128)(2,1)}, bf16[1,2,192,384]{3,2,1,0:T(8,128)(2,1)S(1)}, u32[]{:S(2)}) %copy-start.4) | copy-done | bytes 294936
  50.2 0.0 copy-start.6
  50.2 0.7 %copy-done.6 = bf16[8,32,384]{2,1,0:T(8,128)(2,1)} copy-done((bf16[8,32,384]{2,1,0:T(8,128)(2,1)}, bf16[8,32,384]{2,1,0:T(8,128)(2,1)S(1)}, u32[]{:S(2)}) %copy-start.6) | copy-done | bytes 196632
  50.8 0.0 copy-start.7
  50.8 0.7 %copy-done.7 = f32[2,49,384]{2,1,0:T(8,128)} copy-done((f32[2,49,384]{2,1,0:T(8,128)}, f32[2,49,384]{2,1,0:T(8,128)S(1)}, u32[]{:S(2)}) %copy-start.7) | copy-done | bytes 150552
  51.5 0.0 copy-start.9
  51.5 0.6 %copy-done.9 = bf16[1,2,49,384]{3,2,1,0:T(8,128)(2,1)} copy-done((bf16[1,2,49,384]{3,2,1,0:T(8,128)(2,1)}, bf16[1,2,49,384]{3,2,1,0:T(8,128)(2,1)S(1)}, u32[]{:S(2)}) %copy-start.9) | copy-done | bytes 75288
  52.2 2.6 %finish.1 = (bf16[8,32,384]{2,1,0:T(8,128)(2,1)}, f32[2,192,384]{2,1,0:T(8,128)}, f32[2,49,192]{2,1,0:T(8,128)}) custom-call(bf16[8,32,384]{2,1,0:T(8,128)(2,1)} %copy-done.6, f32[2,384,384]{2,1,0:T(8,128)} %copy-done.1, bf16[1,2,192,384]{3,2,1,0:T(8,128)(2,1)} %copy-done.4, f32[2,49,384]{2,1,0:T(8,128)} %copy-done.7, bf16[1,2,49,384]{3,2,1,0:T(8,128)(2,1)} %copy-done.9), custom_call_target="tpu_custom_call" | custom-call | tf_op jit(solution)/shard_map/finish/pallas_call | solution.py:455
  54.7 1.6 %copy.8 = f32[2,49,192]{2,0,1:T(2,128)} copy(f32[2,49,192]{2,1,0:T(8,128)} %get-tuple-element.21) | data formatting | bytes 150528
Async XLA Ops:
  0.6 2.5 %copy-start = (bf16[2,3,3,384,384]{4,3,2,1,0:T(8,128)(2,1)S(1)}, bf16[2,3,3,384,384]{4,3,2,1,0:T(8,128)(2,1)}, u32[]{:S(2)}) copy-start(bf16[2,3,3,384,384]{4,3,2,1,0:T(8,128)(2,1)} %param.7) | copy-start | bytes 15925252
  3.1 1.1 %copy-start.2 = (bf16[3,1,8,32,384]{4,3,2,1,0:T(8,128)(2,1)S(1)}, bf16[3,1,8,32,384]{4,3,2,1,0:T(8,128)(2,1)}, u32[]{:S(2)}) copy-start(bf16[3,1,8,32,384]{4,3,2,1,0:T(8,128)(2,1)} %param.6) | copy-start | bytes 1769476
  4.2 1.1 %copy-start.3 = (bf16[2,384,384]{2,1,0:T(8,128)(2,1)S(1)}, bf16[2,384,384]{2,1,0:T(8,128)(2,1)}, u32[]{:S(2)}) copy-start(bf16[2,384,384]{2,1,0:T(8,128)(2,1)} %point_hbm.1) | copy-start | bytes 1769476
  5.3 0.9 %copy-start.5 = (bf16[1,1,8,32,384]{4,3,2,1,0:T(8,128)(2,1)S(1)}, bf16[1,1,8,32,384]{4,3,2,1,0:T(8,128)(2,1)}, u32[]{:S(2)}) copy-start(bf16[1,1,8,32,384]{4,3,2,1,0:T(8,128)(2,1)} %param.5) | copy-start | bytes 589828
  6.2 0.9 %copy-start.8 = (f32[2,49,384]{2,0,1:T(2,128)S(1)}, f32[2,49,384]{2,0,1:T(2,128)}, u32[]{:S(2)}) copy-start(f32[2,49,384]{2,0,1:T(2,128)} %param.8) | copy-start | bytes 451588
  48.4 1.0 %copy-start.1 = (f32[2,384,384]{2,1,0:T(8,128)}, f32[2,384,384]{2,1,0:T(8,128)S(1)}, u32[]{:S(2)}) copy-start(f32[2,384,384]{2,1,0:T(8,128)S(1)} %get-tuple-element.12.pg_ref) | copy-start | bytes 3538948
  49.4 0.7 %copy-start.4 = (bf16[1,2,192,384]{3,2,1,0:T(8,128)(2,1)}, bf16[1,2,192,384]{3,2,1,0:T(8,128)(2,1)S(1)}, u32[]{:S(2)}) copy-start(bf16[1,2,192,384]{3,2,1,0:T(8,128)(2,1)S(1)} %get-tuple-element.13.pg_in_ref) | copy-start | bytes 884740
  50.2 0.7 %copy-start.6 = (bf16[8,32,384]{2,1,0:T(8,128)(2,1)}, bf16[8,32,384]{2,1,0:T(8,128)(2,1)S(1)}, u32[]{:S(2)}) copy-start(bf16[8,32,384]{2,1,0:T(8,128)(2,1)S(1)} %get-tuple-element.11.final_in) | copy-start | bytes 589828
  50.8 0.7 %copy-start.7 = (f32[2,49,384]{2,1,0:T(8,128)}, f32[2,49,384]{2,1,0:T(8,128)S(1)}, u32[]{:S(2)}) copy-start(f32[2,49,384]{2,1,0:T(8,128)S(1)} %get-tuple-element.14.dk_ref) | copy-start | bytes 451588
  51.5 0.6 %copy-start.9 = (bf16[1,2,49,384]{3,2,1,0:T(8,128)(2,1)}, bf16[1,2,49,384]{3,2,1,0:T(8,128)(2,1)S(1)}, u32[]{:S(2)}) copy-start(bf16[1,2,49,384]{3,2,1,0:T(8,128)(2,1)S(1)} %get-tuple-element.15.dk_in_ref) | copy-start | bytes 225796

commit v4 on v3

--- a/solution.py
+++ b/solution.py
@@ -24,14 +24,14 @@
     return pl.ds(pl.multiple_of(block * LANES, LANES), LANES)
 
 
-def put_padded(vals, pad_ref, height):
+def put_padded(vals, pad_ref, height, first=0):
     units = vals.shape[0] // (2 * height)
     for block in range(vals.shape[1] // LANES):
         for unit in range(units):
             for half in range(2):
                 at = (2 * unit + half) * height
                 to = (2 * (unit + half * units) + 1) * height
-                pad_ref[block, to : to + height] = vals[at : at + height, lanes(block)]
+                pad_ref[first + block, to : to + height] = vals[at : at + height, lanes(block)]
 
 
 def get_padded(pad_ref, block, height, units):
@@ -43,9 +43,9 @@
     return jnp.concatenate(rows, axis=0)
 
 
-def spread(pad_ref, put, height, units, reach):
+def spread(pad_ref, put, height, units, reach, group=None):
     def one_row(row, carry):
-        for block in range(pad_ref.shape[0]):
+        for block in group or range(pad_ref.shape[0]):
 
             def load(w):
                 return pad_ref[block, pl.ds((2 * w + 1) * height + row - reach, height)]
@@ -120,7 +120,7 @@
     raw, weight, point, raw_sem, weight_sem, point_sem,
     teach, land, send_sem, recv_sem,
     pg_out, pg_land, dk_out, dk_land, swap_send, swap_recv,
-    coef, pad, hpad, src0, src1, src2, win, slope0, slope1, dact0, cur, u_one, resid, gels, grads, sums,
+    coef, pad, hpad, src0, src1, src2, win, slope0, slope1, dact0, cur, acc, u_one, resid, gels, grads, sums,
 ):
     rows, chans = cur.shape
     blocks = chans // LANES
@@ -162,42 +162,81 @@
                 coef[which, block, tap] = jnp.concatenate([line, line], axis=1).astype(BF16)
     sums[...] = jnp.zeros_like(sums)
 
-    def take_raw(tick):
+    def take_raw(tick, group):
         for row in range(height):
-            line = raw[tick, row].astype(F32)
-            for block in range(blocks):
-                pad[block, pl.ds(height + row, 2 * units, stride=pair)] = line[:, lanes(block)]
-
-    def keep_input():
-        for block in range(blocks):
+            for block in group:
+                line = raw[tick, row, :, lanes(block)].astype(F32)
+                pad[block, pl.ds(height + row, 2 * units, stride=pair)] = line
+
+    def keep_input(group):
+        for block in group:
             cur[:, lanes(block)] = get_padded(pad, block, height, units)
-        spread(pad, windows(win, height), height, units, 1)
-
-    def conv(which):
-        parts = [win[down, right * pair : right * pair + rows] for down in range(3) for right in range(3)]
-        return jnp.dot(jnp.concatenate(parts, axis=1), weight[which], preferred_element_type=F32)
-
-    def keep_hidden(hidden):
-        put_padded(jnp.maximum(hidden, 0.0), hpad, height)
+        spread(pad, windows(win, height), height, units, 1, group)
+
+    def half_rows(half):
+        return slice(half * rows // 2, (half + 1) * rows // 2)
+
+    def window(half, down, right, cols):
+        start = right * pair + half * rows // 2
+        return win[down, start : start + rows // 2, cols]
+
+    def first_conv(block, half):
+        spots = [(down, right) for down in range(3) for right in range(3)]
+        left = jnp.concatenate([window(half, down, right, lanes(block)) for down, right in spots], axis=1)
+        starts = [(3 * down + right) * chans + block * LANES for down, right in spots]
+        deep = jnp.concatenate([weight[0, at : at + LANES] for at in starts], axis=0)
+        part = jnp.dot(left, deep, preferred_element_type=F32)
+        acc[half_rows(half)] = part if block == 0 else acc[half_rows(half)] + part
+
+    def second_conv(cols, half, tick):
+        spots = [(down, right) for down in range(3) for right in range(3)]
+        left = jnp.concatenate([window(half, down, right, slice(None)) for down, right in spots], axis=1)
+        part = jnp.dot(left, weight[1, :, cols], preferred_element_type=F32)
+        teach[tick, half_rows(half), cols] = (0.8 * (cur[half_rows(half), cols] + part)).astype(BF16)
+
+    def keep_hidden():
+        put_padded(jnp.maximum(acc[...], 0.0), hpad, height)
         spread(hpad, windows(win, height), height, units, 1)
 
-    def keep_teach(second, tick):
-        teach[tick] = (0.8 * (cur[...] + second)).astype(BF16)
-
-    def relay(tick):
+    early = list(range(max(1, 2 * blocks // 3)))
+    groups = [early, [block for block in range(blocks) if block not in early]]
+    groups = [group for group in groups if group]
+
+    def group_columns(group):
+        return slice(group[0] * LANES, (group[-1] + 1) * LANES)
+
+    def relay(tick, part):
+        cols = group_columns(groups[part])
         return pltpu.make_async_remote_copy(
-            src_ref=teach.at[tick],
-            dst_ref=land.at[tick],
-            send_sem=send_sem.at[tick],
-            recv_sem=recv_sem.at[tick],
+            src_ref=teach.at[tick, :, cols],
+            dst_ref=land.at[tick, :, cols],
+            send_sem=send_sem.at[tick, part],
+            recv_sem=recv_sem.at[tick, part],
             device_id={"section": lax.rem(spot + 1, sections)},
             device_id_type=MESH,
         )
 
-    def send(tick):
+    def send(tick, part):
         @pl.when(spot < sections - 1)
         def _():
-            relay(tick).start()
+            relay(tick, part).start()
+
+    def mix(main, side):
+        done = 0
+        for at, step_of in enumerate(main):
+            upto = len(side) * (at + 1) // len(main)
+            for other in side[done:upto]:
+                other()
+            done = upto
+            step_of()
+
+    def run_first(part, side):
+        main = [functools.partial(first_conv, block, half) for block in groups[part] for half in range(2)]
+        mix(main, side)
+
+    def run_second(part, tick, side):
+        cols = group_columns(groups[part])
+        mix([functools.partial(second_conv, cols, half, tick) for half in range(2)], side)
 
     def back_point(which, tick):
         dgel = lax.dot_general(grads[which, tick], point[which], NT, preferred_element_type=F32)
@@ -240,55 +279,67 @@
         for block in range(blocks):
             dact0[block] = beside(dact[:, lanes(block)], height).astype(BF16)
 
-    def taps_grad(which):
-        for block in range(blocks):
-            part = src2[block, 3, 3 : 3 + units] if which else dact0[block]
-            for row in range(SIDE):
-                strip = srcs[which][block, row]
-                for col in range(SIDE):
-                    prod = strip[col : col + units] * part
-                    size = units
-                    while size > 1:
-                        size //= 2
-                        prod = prod[:size] + prod[size:]
-                    wide = prod[0].astype(F32)
-                    sums[which, block, row, col] += wide[:, :LANES] + wide[:, LANES:]
+    def tap_row(which, block, row):
+        part = src2[block, 3, 3 : 3 + units] if which else dact0[block]
+        strip = srcs[which][block, row]
+        for col in range(SIDE):
+            prod = strip[col : col + units] * part
+            size = units
+            while size > 1:
+                size //= 2
+                prod = prod[:size] + prod[size:]
+            wide = prod[0].astype(F32)
+            sums[which, block, row, col] += wide[:, :LANES] + wide[:, LANES:]
+
+    def tap_rows(which):
+        return [functools.partial(tap_row, which, block, row) for block in range(blocks) for row in range(SIDE)]
+
+    def share_out(steps):
+        cut = [0]
+        for group in groups:
+            cut.append(cut[-1] + len(group) * len(steps) // blocks)
+        return [steps[cut[i] : cut[i + 1]] for i in range(len(groups))]
 
     fetch_pipe.wait()
-    take_raw(0)
-    keep_input()
+    take_raw(0, range(blocks))
+    keep_input(range(blocks))
     fetch_weight[0].wait()
-    keep_hidden(conv(0))
+    for part in range(len(groups)):
+        run_first(part, [])
+    keep_hidden()
     fetch_weight[1].wait()
-    keep_teach(conv(1), 0)
     pl.semaphore_wait(barrier, parties - 1 + (spot < sections - 1).astype(jnp.int32))
-    send(0)
+    for part in range(len(groups)):
+        run_second(part, 0, [])
+        send(0, part)
     fetch_point.wait()
     fetch_fresh.wait()
 
     def tick_body(tick, carry):
         student(tick)
-
-        @pl.when(spot > 0)
-        def _():
-            relay(tick).wait_recv()
-            put_padded(land[tick].astype(F32), pad, height)
-
-        @pl.when(spot == 0)
-        def _():
-            take_raw(tick + 1)
-
-        keep_input()
-        hidden = conv(0)
-        taps_grad(1)
-        keep_hidden(hidden)
-        second = conv(1)
-        taps_grad(0)
-        keep_teach(second, tick + 1)
-
-        @pl.when(tick + 1 < ticks - 1)
-        def _():
-            send(tick + 1)
+        sides = share_out(tap_rows(1))
+        for part, group in enumerate(groups):
+
+            @pl.when(spot > 0)
+            def _():
+                relay(tick, part).wait_recv()
+                put_padded(land[tick, :, group_columns(group)].astype(F32), pad, height, group[0])
+
+            @pl.when(spot == 0)
+            def _():
+                take_raw(tick + 1, group)
+
+            keep_input(group)
+            run_first(part, sides[part])
+        keep_hidden()
+        steps = tap_rows(0)
+        for part in range(len(groups)):
+            many = len(steps) // len(groups)
+            run_second(part, tick + 1, steps[part * many : (part + 1) * many if part + 1 < len(groups) else len(steps)])
+
+            @pl.when(tick + 1 < ticks - 1)
+            def _():
+                send(tick + 1, part)
 
         return carry
 
@@ -328,11 +379,13 @@
         pg_out[which] = total.astype(BF16)
 
     point_grad(1)
-    taps_grad(1)
+    for step_of in tap_rows(1):
+        step_of()
     for hop in range(1, parties):
         swap(hop, 1).start()
     point_grad(0)
-    taps_grad(0)
+    for step_of in tap_rows(0):
+        step_of()
     for hop in range(1, parties):
         swap(hop, 0).start()
     for which in range(2):
@@ -356,7 +409,8 @@
     @pl.when(spot < sections - 1)
     def _():
         for tick in range(ticks - 1):
-            relay(tick).wait_send()
+            for part in range(len(groups)):
+                relay(tick, part).wait_send()
 
 
 def finish_kernel(parties, final_in, pg_ref, pg_in_ref, dk_ref, dk_in_ref, final_ref, point_ref, depth_ref):
@@ -375,7 +429,7 @@
 
             @pl.when(me == party)
             def _():
-                depth_ref[which] = depth[:, party * share : (party + 1) * share]
+                depth_ref[:, which] = depth[:, party * share : (party + 1) * share]
 
 
 def body(pipe_maps, fresh_maps, teacher_weight, student_depth, student_point):
@@ -388,7 +442,7 @@
     sections, parties = lax.axis_size("section"), lax.axis_size("dp")
     share = chans // parties
     peers = max(parties - 1, 1)
-    hbm = pl.BlockSpec(memory_space=pl.ANY)
+    hbm = pl.BlockSpec(memory_space=pltpu.HBM)
     vmem = pl.BlockSpec(memory_space=pltpu.VMEM)
     dma = pltpu.SemaphoreType.DMA
     pad_shape = pltpu.VMEM((blocks, (2 * width + 1) * height, LANES), F32)
@@ -416,8 +470,8 @@
             dma,
             pltpu.VMEM((ticks, rows, chans), BF16),
             pltpu.VMEM((ticks - 1, rows, chans), BF16),
-            dma((ticks - 1,)),
-            dma((ticks - 1,)),
+            dma((ticks - 1, 2)),
+            dma((ticks - 1, 2)),
             pltpu.VMEM((2, chans, chans), BF16),
             pltpu.VMEM((peers, 2, share, chans), BF16),
             pltpu.VMEM((2, taps, chans), BF16),
@@ -434,6 +488,7 @@
             map_shape,
             map_shape,
             pltpu.VMEM((blocks, units, height, 2 * LANES), BF16),
+            map_shape,
             map_shape,
             map_shape,
             map_shape,
@@ -457,13 +512,14 @@
         out_shape=(
             results[0],
             jax.ShapeDtypeStruct((2, share, chans), F32),
-            jax.ShapeDtypeStruct((2, taps, share), F32),
+            jax.ShapeDtypeStruct((taps, 2, share), F32),
         ),
         in_specs=[vmem] * len(outs),
         out_specs=(vmem,) * 3,
+        compiler_params=pltpu.CompilerParams(vmem_limit_bytes=6 << 20),
         name="finish",
     )(*outs)
-    return final[None, None], point_grad.swapaxes(1, 2), depth_grad
+    return final[None, None], point_grad.swapaxes(1, 2), depth_grad.swapaxes(0, 1)
 
 
 def solution(mesh):

time: 56.7 us -> 47.1 us (0.83)
  local copies, waits for them, and re-layouts: 11.8 us -> 6.46 us
  Pallas kernels: 43.9 us -> 39.7 us
    unnamed x21 -> x10, local copies, waits for them, and re-layouts: 11.8 us -> 6.46 us
    pallas_call x1, Pallas kernels: 41.3 us -> 38.5 us  [body(): pl.pallas_call(functools.partial(step_kernel, height, units // 2, ticks,...]
    pallas_call x1, Pallas kernels: 2.59 us -> 1.24 us  [body(): pl.pallas_call(functools.partial(finish_kernel, parties), out_shape=(resu...]
where the time goes in v4:
time: 47.1 us; the launch traced here: 46.8 us
  Pallas kernels  39.7 us (84%)
  local copies, waits for them, and re-layouts  6.46 us (14%)
  between operations  0.65 us (1%)
    pallas_call x1, Pallas kernels, body(): pl.pallas_call(functools.partial(step_kernel, height, units // 2, ticks,...  38.5 us
    unnamed x10, local copies, waits for them, and re-layouts  6.46 us
    pallas_call x1, Pallas kernels, body(): pl.pallas_call(functools.partial(finish_kernel, parties), out_shape=(resu...  1.24 us

profile of v4, /device:TPU:25, one launch (start us, length us, event | category | flops | bytes accessed | tf_op | source)
XLA Modules:
  0.0 46.8 jit_solution(13665386262888296727)
XLA Ops:
  0.6 0.0 copy-start
  0.6 2.5 %copy-done = bf16[2,3,3,384,384]{4,3,2,1,0:T(8,128)(2,1)S(1)} copy-done((bf16[2,3,3,384,384]{4,3,2,1,0:T(8,128)(2,1)S(1)}, bf16[2,3,3,384,384]{4,3,2,1,0:T(8,128)(2,1)}, u32[]{:S(2)}) %copy-start) | copy-done | bytes 5308440
  3.1 0.0 copy-start.1
  3.1 1.1 %copy-done.1 = bf16[3,1,8,32,384]{4,3,2,1,0:T(8,128)(2,1)S(1)} copy-done((bf16[3,1,8,32,384]{4,3,2,1,0:T(8,128)(2,1)S(1)}, bf16[3,1,8,32,384]{4,3,2,1,0:T(8,128)(2,1)}, u32[]{:S(2)}) %copy-start.1) | copy-done | bytes 589848
  4.2 0.0 copy-start.2
  4.2 1.1 %copy-done.2 = bf16[2,384,384]{2,1,0:T(8,128)(2,1)S(1)} copy-done((bf16[2,384,384]{2,1,0:T(8,128)(2,1)S(1)}, bf16[2,384,384]{2,1,0:T(8,128)(2,1)}, u32[]{:S(2)}) %copy-start.2) | copy-done | bytes 589848
  5.3 0.0 copy-start.3
  5.3 0.9 %copy-done.3 = bf16[1,1,8,32,384]{4,3,2,1,0:T(8,128)(2,1)S(1)} copy-done((bf16[1,1,8,32,384]{4,3,2,1,0:T(8,128)(2,1)S(1)}, bf16[1,1,8,32,384]{4,3,2,1,0:T(8,128)(2,1)}, u32[]{:S(2)}) %copy-start.3) | copy-done | bytes 196632
  6.2 0.0 copy-start.4
  6.2 0.9 %copy-done.4 = f32[2,49,384]{2,0,1:T(2,128)S(1)} copy-done((f32[2,49,384]{2,0,1:T(2,128)S(1)}, f32[2,49,384]{2,0,1:T(2,128)}, u32[]{:S(2)}) %copy-start.4) | copy-done | bytes 150552
  7.1 38.5 %step.1 = (bf16[8,32,384]{2,1,0:T(8,128)(2,1)S(1)}, f32[2,384,384]{2,1,0:T(8,128)S(1)}, bf16[1,2,192,384]{3,2,1,0:T(8,128)(2,1)S(1)}, f32[2,49,384]{2,1,0:T(8,128)S(1)}, bf16[1,2,49,384]{3,2,1,0:T(8,128)(2,1)S(1)}) custom-call(bf16[8,32,384]{2,1,0:T(8,128)(2,1)S(1)} %bitcast.9, bf16[3,8,32,384]{3,2,1,0:T(8,128)(2,1)S(1)} %bitcast.8, ...), custom_call_target="tpu_custom_call" | custom-call | tf_op jit(solution)/shard_map/step/pallas_call | solution.py:459
  45.6 1.2 %finish.1 = (bf16[8,32,384]{2,1,0:T(8,128)(2,1)}, f32[2,192,384]{2,1,0:T(8,128)}, f32[49,2,192]{2,1,0:T(2,128)}) custom-call(bf16[8,32,384]{2,1,0:T(8,128)(2,1)S(1)} %get-tuple-element.11.final_in, f32[2,384,384]{2,1,0:T(8,128)S(1)} %get-tuple-element.12.pg_ref, bf16[1,2,192,384]{3,2,1,0:T(8,128)(2,1)S(1)} %get-tuple-element.13.pg_in_ref, ...), custom_call_target="tpu_custom_call" | custom-call | tf_op jit(solution)/shard_map/finish/pallas_call | solution.py:510
Async XLA Ops:
  0.6 2.5 %copy-start = (bf16[2,3,3,384,384]{4,3,2,1,0:T(8,128)(2,1)S(1)}, bf16[2,3,3,384,384]{4,3,2,1,0:T(8,128)(2,1)}, u32[]{:S(2)}) copy-start(bf16[2,3,3,384,384]{4,3,2,1,0:T(8,128)(2,1)} %param.7) | copy-start | bytes 15925252
  3.1 1.1 %copy-start.1 = (bf16[3,1,8,32,384]{4,3,2,1,0:T(8,128)(2,1)S(1)}, bf16[3,1,8,32,384]{4,3,2,1,0:T(8,128)(2,1)}, u32[]{:S(2)}) copy-start(bf16[3,1,8,32,384]{4,3,2,1,0:T(8,128)(2,1)} %param.6) | copy-start | bytes 1769476
  4.2 1.1 %copy-start.2 = (bf16[2,384,384]{2,1,0:T(8,128)(2,1)S(1)}, bf16[2,384,384]{2,1,0:T(8,128)(2,1)}, u32[]{:S(2)}) copy-start(bf16[2,384,384]{2,1,0:T(8,128)(2,1)} %point_hbm.1) | copy-start | bytes 1769476
  5.3 0.9 %copy-start.3 = (bf16[1,1,8,32,384]{4,3,2,1,0:T(8,128)(2,1)S(1)}, bf16[1,1,8,32,384]{4,3,2,1,0:T(8,128)(2,1)}, u32[]{:S(2)}) copy-start(bf16[1,1,8,32,384]{4,3,2,1,0:T(8,128)(2,1)} %param.5) | copy-start | bytes 589828
  6.2 0.9 %copy-start.4 = (f32[2,49,384]{2,0,1:T(2,128)S(1)}, f32[2,49,384]{2,0,1:T(2,128)}, u32[]{:S(2)}) copy-start(f32[2,49,384]{2,0,1:T(2,128)} %param.8) | copy-start | bytes 451588

commit v5 on v4

--- a/solution.py
+++ b/solution.py
@@ -115,9 +115,9 @@
 
 def step_kernel(
     height, step, ticks, sections, parties,
-    pipe_hbm, fresh_hbm, weight_hbm, taps_ref, point_hbm,
+    pipe_hbm, fresh_hbm, weight_hbm, taps_hbm, point_hbm,
     final_ref, pg_ref, pg_in_ref, dk_ref, dk_in_ref,
-    raw, weight, point, raw_sem, weight_sem, point_sem,
+    raw, weight, taps_ref, point, raw_sem, weight_sem, taps_sem, point_sem,
     teach, land, send_sem, recv_sem,
     pg_out, pg_land, dk_out, dk_land, swap_send, swap_recv,
     coef, pad, hpad, src0, src1, src2, win, slope0, slope1, dact0, cur, acc, u_one, resid, gels, grads, sums,
@@ -143,8 +143,9 @@
     fetch_pipe = pltpu.make_async_copy(pipe_hbm, raw.at[0], raw_sem.at[0])
     fetch_fresh = pltpu.make_async_copy(fresh_hbm, raw.at[pl.ds(1, ticks - 1)], raw_sem.at[1])
     fetch_weight = [pltpu.make_async_copy(weight_hbm.at[i], weight.at[i], weight_sem.at[i]) for i in range(2)]
+    fetch_taps = pltpu.make_async_copy(taps_hbm, taps_ref, taps_sem)
     fetch_point = pltpu.make_async_copy(point_hbm, point, point_sem)
-    for fetch in (fetch_pipe, fetch_weight[0], fetch_weight[1], fetch_point, fetch_fresh):
+    for fetch in (fetch_pipe, fetch_weight[0], fetch_weight[1], fetch_taps, fetch_point, fetch_fresh):
         fetch.start()
 
     def span(index):
@@ -155,11 +156,6 @@
         for at in range(0, pad.shape[1], pair):
             pad[block, at : at + height] = zero
             hpad[block, at : at + height] = zero
-    for which in range(2):
-        for block in range(blocks):
-            for tap in range(SIDE * SIDE):
-                line = jnp.broadcast_to(taps_ref[tap, which : which + 1, lanes(block)], (height, LANES))
-                coef[which, block, tap] = jnp.concatenate([line, line], axis=1).astype(BF16)
     sums[...] = jnp.zeros_like(sums)
 
     def take_raw(tick, group):
@@ -312,6 +308,12 @@
     for part in range(len(groups)):
         run_second(part, 0, [])
         send(0, part)
+    fetch_taps.wait()
+    for which in range(2):
+        for block in range(blocks):
+            for tap in range(SIDE * SIDE):
+                line = jnp.broadcast_to(taps_ref[tap, which : which + 1, lanes(block)], (height, LANES))
+                coef[which, block, tap] = jnp.concatenate([line, line], axis=1).astype(BF16)
     fetch_point.wait()
     fetch_fresh.wait()
 
@@ -459,14 +461,16 @@
     outs = pl.pallas_call(
         functools.partial(step_kernel, height, units // 2, ticks, sections, parties),
         out_shape=results,
-        in_specs=[hbm, hbm, hbm, vmem, hbm],
+        in_specs=[hbm] * 5,
         out_specs=(vmem,) * len(results),
         scratch_shapes=[
             pltpu.VMEM((ticks, height, width, chans), BF16),
             pltpu.VMEM((2, 9 * chans, chans), BF16),
+            pltpu.VMEM((taps, 2, chans), F32),
             pltpu.VMEM((2, chans, chans), BF16),
             dma((2,)),
             dma((2,)),
+            dma,
             dma,
             pltpu.VMEM((ticks, rows, chans), BF16),
             pltpu.VMEM((ticks - 1, rows, chans), BF16),
@@ -501,11 +505,11 @@
         ),
         name="step",
     )(
-        pipe_maps[0, 0],
-        fresh_maps[:, 0],
-        teacher_weight.reshape(2, 9 * chans, chans),
-        student_depth.swapaxes(0, 1),
-        student_point,
+        pltpu.with_memory_space_constraint(pipe_maps[0, 0], pltpu.HBM),
+        pltpu.with_memory_space_constraint(fresh_maps[:, 0], pltpu.HBM),
+        pltpu.with_memory_space_constraint(teacher_weight.reshape(2, 9 * chans, chans), pltpu.HBM),
+        pltpu.with_memory_space_constraint(student_depth.swapaxes(0, 1), pltpu.HBM),
+        pltpu.with_memory_space_constraint(student_point, pltpu.HBM),
     )
     final, point_grad, depth_grad = pl.pallas_call(
         functools.partial(finish_kernel, parties),

time: 47.1 us -> 41.2 us (0.87)
  local copies, waits for them, and re-layouts: 6.46 us -> 0 us
  Pallas kernels: 39.7 us -> 40.4 us
    unnamed x10 -> x0, local copies, waits for them, and re-layouts: 6.46 us -> none
    pallas_call x1, Pallas kernels: 38.5 us -> 39.2 us  [body(): pl.pallas_call(functools.partial(step_kernel, height, units // 2, ticks,...]
where the time goes in v5:
time: 41.2 us; the launch traced here: 41.1 us
  Pallas kernels  40.4 us (98%)
  between operations  0.64 us (2%)
    pallas_call x1, Pallas kernels, body(): pl.pallas_call(functools.partial(step_kernel, height, units // 2, ticks,...  39.2 us
    pallas_call x1, Pallas kernels, body(): pl.pallas_call(functools.partial(finish_kernel, parties), out_shape=(resu...  1.24 us

profile of v5, /device:TPU:25, one launch (start us, length us, event | category | flops | bytes accessed | tf_op | source)
XLA Modules:
  0.0 41.1 jit_solution(9424546679868251975)
XLA Ops:
  0.6 39.2 %step.1 = (bf16[8,32,384]{2,1,0:T(8,128)(2,1)S(1)}, f32[2,384,384]{2,1,0:T(8,128)S(1)}, bf16[1,2,192,384]{3,2,1,0:T(8,128)(2,1)S(1)}, f32[2,49,384]{2,1,0:T(8,128)S(1)}, bf16[1,2,49,384]{3,2,1,0:T(8,128)(2,1)S(1)}) custom-call(bf16[8,32,384]{2,1,0:T(8,128)(2,1)} %bitcast.9, bf16[3,8,32,384]{3,2,1,0:T(8,128)(2,1)} %bitcast.8, bf16[2,3456,384]{2,1,0:T(8,128)(2,1)} %bitcast.7, ...), custom_call_target="tpu_custom_call" | custom-call | tf_op jit(solution)/shard_map/step/pallas_call | solution.py:461
  39.8 1.2 %finish.1 = (bf16[8,32,384]{2,1,0:T(8,128)(2,1)}, f32[2,192,384]{2,1,0:T(8,128)}, f32[49,2,192]{2,1,0:T(2,128)}) custom-call(bf16[8,32,384]{2,1,0:T(8,128)(2,1)S(1)} %get-tuple-element.11.final_in, f32[2,384,384]{2,1,0:T(8,128)S(1)} %get-tuple-element.12.pg_ref, bf16[1,2,192,384]{3,2,1,0:T(8,128)(2,1)S(1)} %get-tuple-element.13.pg_in_ref, ...), custom_call_target="tpu_custom_call" | custom-call | tf_op jit(solution)/shard_map/finish/pallas_call | solution.py:514

commit v6 on v5

--- a/solution.py
+++ b/solution.py
@@ -157,6 +157,7 @@
             pad[block, at : at + height] = zero
             hpad[block, at : at + height] = zero
     sums[...] = jnp.zeros_like(sums)
+    pg_ref[...] = jnp.zeros_like(pg_ref)
 
     def take_raw(tick, group):
         for row in range(height):
@@ -212,11 +213,6 @@
             device_id_type=MESH,
         )
 
-    def send(tick, part):
-        @pl.when(spot < sections - 1)
-        def _():
-            relay(tick, part).start()
-
     def mix(main, side):
         done = 0
         for at, step_of in enumerate(main):
@@ -230,9 +226,19 @@
         main = [functools.partial(first_conv, block, half) for block in groups[part] for half in range(2)]
         mix(main, side)
 
-    def run_second(part, tick, side):
-        cols = group_columns(groups[part])
-        mix([functools.partial(second_conv, cols, half, tick) for half in range(2)], side)
+    def split(steps, weights):
+        cut = [len(steps) * sum(weights[:at]) // sum(weights) for at in range(len(weights) + 1)]
+        return [steps[cut[at] : cut[at + 1]] for at in range(len(weights))]
+
+    def run_second(tick, side, sends):
+        sides = split(side, [1] * len(groups))
+        for part, group in enumerate(groups):
+            cols = group_columns(group)
+            mix([functools.partial(second_conv, cols, half, tick) for half in range(2)], sides[part])
+
+            @pl.when(sends)
+            def _():
+                relay(tick, part).start()
 
     def back_point(which, tick):
         dgel = lax.dot_general(grads[which, tick], point[which], NT, preferred_element_type=F32)
@@ -247,8 +253,11 @@
             gels[which, tick, span(index), columns(block)] = gel.astype(BF16)
             return carry
 
-        lax.fori_loop(0, blocks * chunks, chunk, 0)
+        lax.fori_loop(0, blocks * chunks, chunk, 0, unroll=blocks)
         return jnp.dot(gels[which, tick], point[which], preferred_element_type=F32)
+
+    def point_grad(which, tick):
+        pg_ref[which] += lax.dot_general(grads[which, tick], gels[which, tick], TN, preferred_element_type=F32)
 
     def student(tick):
         spread(pad, strips(src0), height, units, 3)
@@ -270,10 +279,12 @@
             grads[0, tick, span(index), columns(block)] = back.astype(BF16)
             return carry
 
-        lax.fori_loop(0, blocks * chunks, chunk_back, 0)
+        lax.fori_loop(0, blocks * chunks, chunk_back, 0, unroll=blocks)
         dact = back_point(0, tick)
         for block in range(blocks):
             dact0[block] = beside(dact[:, lanes(block)], height).astype(BF16)
+        point_grad(1, tick)
+        point_grad(0, tick)
 
     def tap_row(which, block, row):
         part = src2[block, 3, 3 : 3 + units] if which else dact0[block]
@@ -290,12 +301,6 @@
     def tap_rows(which):
         return [functools.partial(tap_row, which, block, row) for block in range(blocks) for row in range(SIDE)]
 
-    def share_out(steps):
-        cut = [0]
-        for group in groups:
-            cut.append(cut[-1] + len(group) * len(steps) // blocks)
-        return [steps[cut[i] : cut[i + 1]] for i in range(len(groups))]
-
     fetch_pipe.wait()
     take_raw(0, range(blocks))
     keep_input(range(blocks))
@@ -305,9 +310,7 @@
     keep_hidden()
     fetch_weight[1].wait()
     pl.semaphore_wait(barrier, parties - 1 + (spot < sections - 1).astype(jnp.int32))
-    for part in range(len(groups)):
-        run_second(part, 0, [])
-        send(0, part)
+    run_second(0, [], spot < sections - 1)
     fetch_taps.wait()
     for which in range(2):
         for block in range(blocks):
@@ -319,7 +322,7 @@
 
     def tick_body(tick, carry):
         student(tick)
-        sides = share_out(tap_rows(1))
+        sides = split(tap_rows(1), [len(group) for group in groups])
         for part, group in enumerate(groups):
 
             @pl.when(spot > 0)
@@ -334,15 +337,7 @@
             keep_input(group)
             run_first(part, sides[part])
         keep_hidden()
-        steps = tap_rows(0)
-        for part in range(len(groups)):
-            many = len(steps) // len(groups)
-            run_second(part, tick + 1, steps[part * many : (part + 1) * many if part + 1 < len(groups) else len(steps)])
-
-            @pl.when(tick + 1 < ticks - 1)
-            def _():
-                send(tick + 1, part)
-
+        run_second(tick + 1, tap_rows(0), (spot < sections - 1) & (tick + 1 < ticks - 1))
         return carry
 
     lax.fori_loop(0, ticks - 1, tick_body, 0)
@@ -374,22 +369,13 @@
             device_id_type=MESH,
         )
 
-    def point_grad(which):
-        up = grads[which].reshape(ticks * rows, chans)
-        total = lax.dot_general(up, gels[which].reshape(ticks * rows, chans), TN, preferred_element_type=F32)
-        pg_ref[which] = total
-        pg_out[which] = total.astype(BF16)
-
-    point_grad(1)
-    for step_of in tap_rows(1):
-        step_of()
-    for hop in range(1, parties):
-        swap(hop, 1).start()
-    point_grad(0)
-    for step_of in tap_rows(0):
-        step_of()
-    for hop in range(1, parties):
-        swap(hop, 0).start()
+    pg_out[...] = pg_ref[...].astype(BF16)
+    for which in (1, 0):
+        for hop in range(1, parties):
+            swap(hop, which).start()
+    for which in (1, 0):
+        for step_of in tap_rows(which):
+            step_of()
     for which in range(2):
         for block in range(blocks):
             for row in range(SIDE):

time: 41.2 us -> 40.3 us (0.978)
  Pallas kernels: 40.4 us -> 39.5 us
    pallas_call x1, Pallas kernels: 39.2 us -> 38.2 us  [body(): pl.pallas_call(functools.partial(step_kernel, height, units // 2, ticks,...]
where the time goes in v6:
time: 40.3 us; the launch traced here: 40.1 us
  Pallas kernels  39.5 us (98%)
  between operations  0.64 us (2%)
    pallas_call x1, Pallas kernels, body(): pl.pallas_call(functools.partial(step_kernel, height, units // 2, ticks,...  38.2 us
    pallas_call x1, Pallas kernels, body(): pl.pallas_call(functools.partial(finish_kernel, parties), out_shape=(resu...  1.24 us

profile of v6, /device:TPU:25, one launch (start us, length us, event | category | flops | bytes accessed | tf_op | source)
XLA Modules:
  0.0 40.1 jit_solution(15044381770010316069)
XLA Ops:
  0.6 38.2 %step.1 = (bf16[8,32,384]{2,1,0:T(8,128)(2,1)S(1)}, f32[2,384,384]{2,1,0:T(8,128)S(1)}, bf16[1,2,192,384]{3,2,1,0:T(8,128)(2,1)S(1)}, f32[2,49,384]{2,1,0:T(8,128)S(1)}, bf16[1,2,49,384]{3,2,1,0:T(8,128)(2,1)S(1)}) custom-call(bf16[8,32,384]{2,1,0:T(8,128)(2,1)} %bitcast.9, bf16[3,8,32,384]{3,2,1,0:T(8,128)(2,1)} %bitcast.8, bf16[2,3456,384]{2,1,0:T(8,128)(2,1)} %bitcast.7, ...), custom_call_target="tpu_custom_call" | custom-call | tf_op jit(solution)/shard_map/step/pallas_call | solution.py:447
  38.9 1.2 %finish.1 = (bf16[8,32,384]{2,1,0:T(8,128)(2,1)}, f32[2,192,384]{2,1,0:T(8,128)}, f32[49,2,192]{2,1,0:T(2,128)}) custom-call(bf16[8,32,384]{2,1,0:T(8,128)(2,1)S(1)} %get-tuple-element.11.final_in, f32[2,384,384]{2,1,0:T(8,128)S(1)} %get-tuple-element.12.pg_ref, bf16[1,2,192,384]{3,2,1,0:T(8,128)(2,1)S(1)} %get-tuple-element.13.pg_in_ref, ...), custom_call_target="tpu_custom_call" | custom-call | tf_op jit(solution)/shard_map/finish/pallas_call | solution.py:500
